TPU v7x, 512 devices: a whole 4x8x8 slice. The times are simulated.
512 devices in a mesh: pipe: 16 (over z, core), expert: 8 (over y), dp: 4 (over x).
Axes of the slice: x: 4, y: 8, z: 8, core: 2. Of those that a mesh axis runs over, the one named last changes fastest.
Arguments:
- tokens: bfloat16 [8, 8, 16, 6144], P(None, 'expert', None, 'dp'), may hold values from -8 to 8
- norm_gain: float32 [6144], P('dp'), may hold values from 0.5 to 1.5
- up_w: bfloat16 [8, 6144, 8192], P('expert', 'dp', 'pipe'), may hold values from -0.078125 to 0.078125
- down_w: bfloat16 [8, 8192, 6144], P('expert', 'pipe', 'dp'), may hold values from -0.0625 to 0.0625
- expert_ids: int32 [8, 8, 16, 2], P(None, 'expert'), may hold values from 0 to 7, all different within a row; in each aligned block of 16 rows (0 to 15, 16 to 31, ..., all dimensions but the last counted through in order) at most 6 rows name the same one
- gate_gap: float32 [8, 8, 16], P(None, 'expert'), may hold values from 0 to 2.5
Outputs:
- result: bfloat16 [8, 8, 16, 6144], P(None, 'expert', None, ('dp', 'pipe'))
Inputs may be any that keep to these rules, and one draw needn't show every extreme that they name: `expert_ids`: each token names 2 different experts. Of the 16 tokens of one micro-batch and one index along the second dimension (an aligned block of 16 rows), at most 6 name any one expert.
All inputs are finite; a program needn't handle non-finite values.
Results may differ from a plain program's by a relative error of at most 0.0095.
Values may be sent and summed in bfloat16 or wider, within the bound.
A program may use at most 64 MiB of HBM per device.

v0:
```python
import jax
import jax.numpy as jnp
from jax import lax
from jax.sharding import PartitionSpec as P


def shifted_2(value, axis, steps):
    count = lax.axis_size(axis)
    initial, last = (max(0, -steps), min(count, count - steps))
    return lax.ppermute(value, axis, [(source, source + steps) for source in range(initial, last)])


def make_slots(member, capacity):
    slot_rank = jnp.cumsum(member, axis=-1) - member
    slot_index = jnp.arange(capacity, dtype=jnp.int32)
    return (member[..., None, :] == 1) & (slot_rank[..., None, :] == slot_index[:, None])


def on_device(tokens, norm_gain, up_w, down_w, expert_ids, gate_gap):
    segments = lax.axis_size("pipe")
    my_segment = lax.axis_index("pipe")
    experts = lax.axis_size("expert")
    micro_count = tokens.shape[0]
    row_count = tokens.shape[2]
    quarter = tokens.shape[3]
    model_width = quarter * lax.axis_size("dp")
    capacity = max(2, min(row_count, 3 * row_count // experts))
    state_wide = tokens[:, 0].astype(jnp.float32)
    square_sum = lax.psum(jnp.sum(state_wide * state_wide, axis=-1), "dp")
    scale_rows = lax.rsqrt(square_sum / model_width + 1e-05)
    normed = (state_wide * scale_rows[..., None] * norm_gain).astype(jnp.bfloat16)
    chosen = expert_ids[:, 0]
    first_share = jax.nn.sigmoid(gate_gap[:, 0])
    expert_iota = jnp.arange(experts, dtype=jnp.int32)
    hit_mask = chosen[..., None] == expert_iota
    member = jnp.swapaxes(jnp.any(hit_mask, axis=2).astype(jnp.int32), 1, 2)
    slot_table = make_slots(member, capacity)
    outgoing = jnp.einsum(
        "mecr,mrd->emcd",
        slot_table.astype(jnp.bfloat16),
        normed,
        preferred_element_type=jnp.float32,
    ).astype(jnp.bfloat16)
    w_up = up_w[0]
    w_down = down_w[0]
    received = lax.all_to_all(outgoing, "expert", split_axis=0, concat_axis=0, tiled=True)
    src_count, item_count, slot_count, feat_count = received.shape
    flat_rows = received.reshape(src_count * item_count * slot_count, feat_count)
    partial_value = jnp.dot(flat_rows, w_up, preferred_element_type=jnp.float32)
    gate_total = lax.psum(partial_value, "dp")
    hidden = jax.nn.silu(gate_total).astype(jnp.bfloat16)
    expert_out = jnp.dot(hidden, w_down, preferred_element_type=jnp.float32).astype(jnp.bfloat16)
    expert_out = expert_out.reshape(src_count, item_count, slot_count, feat_count)
    returned = lax.all_to_all(expert_out, "expert", split_axis=0, concat_axis=0, tiled=True)
    weight = jnp.where(hit_mask[:, :, 0], first_share[..., None], 0.0) + jnp.where(
        hit_mask[:, :, 1], 1.0 - first_share[..., None], 0.0
    )
    placed = slot_table.astype(jnp.float32) * jnp.swapaxes(weight, 1, 2)[:, :, None, :]
    contrib = jnp.einsum(
        "mecr,emcd->mrd", placed, returned.astype(jnp.float32), precision=lax.Precision.HIGHEST
    )

    def advance(moment, state_pair):
        arriving, finished = state_pair
        micro_index = moment - my_segment
        is_live = (micro_index >= 0) & (micro_index < micro_count)
        micro_index = jnp.clip(micro_index, 0, micro_count - 1)
        own_part = lax.dynamic_index_in_dim(contrib, micro_index, 0, keepdims=False)
        carried = arriving + jnp.where(is_live, own_part, 0.0)
        updated = lax.dynamic_update_slice_in_dim(finished, carried[None], micro_index, 0)
        finished = jnp.where(is_live & (my_segment == segments - 1), updated, finished)
        shifted = shifted_2(carried, "pipe", 1)
        return (shifted, finished)

    zeros_rows = jnp.zeros((row_count, quarter), jnp.float32)
    finished = jnp.zeros((micro_count, row_count, quarter), jnp.float32)
    total_steps = micro_count + segments - 1
    arriving, finished = lax.fori_loop(0, total_steps, advance, (zeros_rows, finished))
    last_total = jnp.where(my_segment == segments - 1, state_wide + finished, 0.0)
    result = lax.psum_scatter(
        last_total.astype(jnp.bfloat16), "pipe", scatter_dimension=2, tiled=True
    )
    return result[:, None]


def solution(mesh):
    return jax.shard_map(
        on_device,
        mesh=mesh,
        in_specs=(
            P(None, "expert", None, "dp"),
            P("dp"),
            P("expert", "dp", "pipe"),
            P("expert", "pipe", "dp"),
            P(None, "expert", None, None),
            P(None, "expert", None),
        ),
        out_specs=P(None, "expert", None, ("dp", "pipe")),
        check_vma=False,
    )
```

profile of v0, /device:TPU:1, one launch (start us, length us, event | category | flops | bytes accessed | tf_op | source)
XLA Modules:
  0.0 418.3 jit_solution(2274408692243849220)
XLA Ops:
  9.9 9.3 %psum.14 = f32[8,16]{1,0:T(8,128)S(1)} all-reduce(f32[8,16]{1,0:T(8,128)S(1)} %fusion.6), channel_id=1, replica_groups=mesh['pipe'=16,'expert'=8,'dp'=4] {'dp'}, use_global_device_ids=true, to_apply=%region_3.0 | all-reduce | flops 128 | bytes 1024 | tf_op jit(solution)/shard_map/psum | solution.py:29
  21.4 34.6 %all_to_all.10 = bf16[8,8,6,1536]{3,1,2,0:T(8,128)(2,1)S(1)} all-to-all(bf16[8,8,6,1536]{3,1,2,0:T(8,128)(2,1)S(1)} %copy.25), channel_id=1, replica_groups=mesh['pipe'=16,'expert'=8,'dp'=4] {'expert'}, dimensions={0} | all-to-all | bytes 2359296 | tf_op jit(solution)/shard_map/all_to_all | solution.py:46
  57.6 3.4 fusion.3
  61.1 54.5 %all-reduce.2.cloned.1.call-done = f32[384,512]{1,0:T(8,128)} async-done(((f32[384,512]{1,0:T(8,128)}), f32[384,512]{1,0:T(8,128)}) %all-reduce.2.cloned.1.call-update) | async-done | bytes 786448 | tf_op jit(solution)/shard_map/psum | solution.py:50
  115.6 3.0 convolution_convert_fusion
  118.5 2.2 reshape.38
  122.1 6.7 %all-to-all-start.1 = ((bf16[8,8,6,1536]{3,1,2,0:T(8,128)(2,1)}), bf16[8,8,6,1536]{3,1,2,0:T(8,128)(2,1)S(1)}, u32[]{:S(2)}, u32[]{:S(2)}) async-start(bf16[8,8,6,1536]{3,1,2,0:T(8,128)(2,1)} %copy.27), calls=%async_computation.1 | async-start | bytes 2359296 | tf_op jit(solution)/shard_map/all_to_all | solution.py:54
  128.9 31.8 %all-to-all-done.1 = bf16[8,8,6,1536]{3,1,2,0:T(8,128)(2,1)S(1)} async-done(((bf16[8,8,6,1536]{3,1,2,0:T(8,128)(2,1)}), bf16[8,8,6,1536]{3,1,2,0:T(8,128)(2,1)S(1)}, u32[]{:S(2)}, u32[]{:S(2)}) %all-to-all-start.1) | async-done | bytes 1179680 | tf_op jit(solution)/shard_map/all_to_all | solution.py:54
  160.7 2.6 convolution_bitcast_fusion
  163.4 166.5 %while.16 = (s32[]{:T(128)}, f32[16,1536]{1,0:T(8,128)S(1)}, f32[8,16,1536]{2,1,0:T(8,128)S(1)}, s32[]{:T(128)}, f32[8,16,1536]{2,1,0:T(8,128)}, /*index=5*/pred...) while((s32[]{:T(128)}, f32[16,1536]{1,0:T(8,128)S(1)}, f32[8,16,1536]{2,1,0:T(8,128)S(1)}, s32[]{:T(128)}, ...), condition=%wide.region_6.7_spmd, body=%wide.region_5.6_spmd.sunk | while | flops 73737 | bytes 884943 | solution.py:78
  164.4 3.8 collective-permute-start
  170.7 4.3 %collective-permute-start = (f32[16,1536]{1,0:T(8,128)S(1)}, f32[16,1536]{1,0:T(8,128)S(1)}, u32[]{:S(2)}, u32[]{:S(2)}) collective-permute-start(f32[16,1536]{1,0:T(8,128)S(1)} %get-tuple-element.180), channel_id=1, source_target_pairs={{0,32},{32,64},{64,96},{96,128},{128,160},{160,192},{192,224},{224... | collective-permute-start | bytes 294920 | tf_op jit(solution)/shard_map/while/body/eval_jaxpr/ppermute | solution.py:10
  177.6 4.3 %collective-permute-start = (f32[16,1536]{1,0:T(8,128)S(1)}, f32[16,1536]{1,0:T(8,128)S(1)}, u32[]{:S(2)}, u32[]{:S(2)}) collective-permute-start(f32[16,1536]{1,0:T(8,128)S(1)} %get-tuple-element.180), channel_id=1, source_target_pairs={{0,32},{32,64},{64,96},{96,128},{128,160},{160,192},{192,224},{224... | collective-permute-start | bytes 294920 | tf_op jit(solution)/shard_map/while/body/eval_jaxpr/ppermute | solution.py:10
  181.9 1.6 collective-permute-done
  184.5 4.3 %collective-permute-start = (f32[16,1536]{1,0:T(8,128)S(1)}, f32[16,1536]{1,0:T(8,128)S(1)}, u32[]{:S(2)}, u32[]{:S(2)}) collective-permute-start(f32[16,1536]{1,0:T(8,128)S(1)} %get-tuple-element.180), channel_id=1, source_target_pairs={{0,32},{32,64},{64,96},{96,128},{128,160},{160,192},{192,224},{224... | collective-permute-start | bytes 294920 | tf_op jit(solution)/shard_map/while/body/eval_jaxpr/ppermute | solution.py:10
  188.8 1.6 collective-permute-done
  191.3 4.3 %collective-permute-start = (f32[16,1536]{1,0:T(8,128)S(1)}, f32[16,1536]{1,0:T(8,128)S(1)}, u32[]{:S(2)}, u32[]{:S(2)}) collective-permute-start(f32[16,1536]{1,0:T(8,128)S(1)} %get-tuple-element.180), channel_id=1, source_target_pairs={{0,32},{32,64},{64,96},{96,128},{128,160},{160,192},{192,224},{224... | collective-permute-start | bytes 294920 | tf_op jit(solution)/shard_map/while/body/eval_jaxpr/ppermute | solution.py:10
  195.6 1.6 collective-permute-done
  198.2 4.3 %collective-permute-start = (f32[16,1536]{1,0:T(8,128)S(1)}, f32[16,1536]{1,0:T(8,128)S(1)}, u32[]{:S(2)}, u32[]{:S(2)}) collective-permute-start(f32[16,1536]{1,0:T(8,128)S(1)} %get-tuple-element.180), channel_id=1, source_target_pairs={{0,32},{32,64},{64,96},{96,128},{128,160},{160,192},{192,224},{224... | collective-permute-start | bytes 294920 | tf_op jit(solution)/shard_map/while/body/eval_jaxpr/ppermute | solution.py:10
  205.0 4.3 %collective-permute-start = (f32[16,1536]{1,0:T(8,128)S(1)}, f32[16,1536]{1,0:T(8,128)S(1)}, u32[]{:S(2)}, u32[]{:S(2)}) collective-permute-start(f32[16,1536]{1,0:T(8,128)S(1)} %get-tuple-element.180), channel_id=1, source_target_pairs={{0,32},{32,64},{64,96},{96,128},{128,160},{160,192},{192,224},{224... | collective-permute-start | bytes 294920 | tf_op jit(solution)/shard_map/while/body/eval_jaxpr/ppermute | solution.py:10
  211.9 4.3 %collective-permute-start = (f32[16,1536]{1,0:T(8,128)S(1)}, f32[16,1536]{1,0:T(8,128)S(1)}, u32[]{:S(2)}, u32[]{:S(2)}) collective-permute-start(f32[16,1536]{1,0:T(8,128)S(1)} %get-tuple-element.180), channel_id=1, source_target_pairs={{0,32},{32,64},{64,96},{96,128},{128,160},{160,192},{192,224},{224... | collective-permute-start | bytes 294920 | tf_op jit(solution)/shard_map/while/body/eval_jaxpr/ppermute | solution.py:10
  216.2 1.6 collective-permute-done
  218.7 4.3 %collective-permute-start = (f32[16,1536]{1,0:T(8,128)S(1)}, f32[16,1536]{1,0:T(8,128)S(1)}, u32[]{:S(2)}, u32[]{:S(2)}) collective-permute-start(f32[16,1536]{1,0:T(8,128)S(1)} %get-tuple-element.180), channel_id=1, source_target_pairs={{0,32},{32,64},{64,96},{96,128},{128,160},{160,192},{192,224},{224... | collective-permute-start | bytes 294920 | tf_op jit(solution)/shard_map/while/body/eval_jaxpr/ppermute | solution.py:10
  223.0 1.6 collective-permute-done
  225.6 4.3 %collective-permute-start = (f32[16,1536]{1,0:T(8,128)S(1)}, f32[16,1536]{1,0:T(8,128)S(1)}, u32[]{:S(2)}, u32[]{:S(2)}) collective-permute-start(f32[16,1536]{1,0:T(8,128)S(1)} %get-tuple-element.180), channel_id=1, source_target_pairs={{0,32},{32,64},{64,96},{96,128},{128,160},{160,192},{192,224},{224... | collective-permute-start | bytes 294920 | tf_op jit(solution)/shard_map/while/body/eval_jaxpr/ppermute | solution.py:10
  229.9 1.6 collective-permute-done
  232.4 4.3 %collective-permute-start = (f32[16,1536]{1,0:T(8,128)S(1)}, f32[16,1536]{1,0:T(8,128)S(1)}, u32[]{:S(2)}, u32[]{:S(2)}) collective-permute-start(f32[16,1536]{1,0:T(8,128)S(1)} %get-tuple-element.180), channel_id=1, source_target_pairs={{0,32},{32,64},{64,96},{96,128},{128,160},{160,192},{192,224},{224... | collective-permute-start | bytes 294920 | tf_op jit(solution)/shard_map/while/body/eval_jaxpr/ppermute | solution.py:10
  239.3 4.3 %collective-permute-start = (f32[16,1536]{1,0:T(8,128)S(1)}, f32[16,1536]{1,0:T(8,128)S(1)}, u32[]{:S(2)}, u32[]{:S(2)}) collective-permute-start(f32[16,1536]{1,0:T(8,128)S(1)} %get-tuple-element.180), channel_id=1, source_target_pairs={{0,32},{32,64},{64,96},{96,128},{128,160},{160,192},{192,224},{224... | collective-permute-start | bytes 294920 | tf_op jit(solution)/shard_map/while/body/eval_jaxpr/ppermute | solution.py:10
  246.1 4.3 %collective-permute-start = (f32[16,1536]{1,0:T(8,128)S(1)}, f32[16,1536]{1,0:T(8,128)S(1)}, u32[]{:S(2)}, u32[]{:S(2)}) collective-permute-start(f32[16,1536]{1,0:T(8,128)S(1)} %get-tuple-element.180), channel_id=1, source_target_pairs={{0,32},{32,64},{64,96},{96,128},{128,160},{160,192},{192,224},{224... | collective-permute-start | bytes 294920 | tf_op jit(solution)/shard_map/while/body/eval_jaxpr/ppermute | solution.py:10
  250.5 1.6 collective-permute-done
  253.0 4.3 %collective-permute-start = (f32[16,1536]{1,0:T(8,128)S(1)}, f32[16,1536]{1,0:T(8,128)S(1)}, u32[]{:S(2)}, u32[]{:S(2)}) collective-permute-start(f32[16,1536]{1,0:T(8,128)S(1)} %get-tuple-element.180), channel_id=1, source_target_pairs={{0,32},{32,64},{64,96},{96,128},{128,160},{160,192},{192,224},{224... | collective-permute-start | bytes 294920 | tf_op jit(solution)/shard_map/while/body/eval_jaxpr/ppermute | solution.py:10
  257.3 1.6 collective-permute-done
  259.8 4.3 %collective-permute-start = (f32[16,1536]{1,0:T(8,128)S(1)}, f32[16,1536]{1,0:T(8,128)S(1)}, u32[]{:S(2)}, u32[]{:S(2)}) collective-permute-start(f32[16,1536]{1,0:T(8,128)S(1)} %get-tuple-element.180), channel_id=1, source_target_pairs={{0,32},{32,64},{64,96},{96,128},{128,160},{160,192},{192,224},{224... | collective-permute-start | bytes 294920 | tf_op jit(solution)/shard_map/while/body/eval_jaxpr/ppermute | solution.py:10
  266.7 5.2 %collective-permute-start = (f32[16,1536]{1,0:T(8,128)S(1)}, f32[16,1536]{1,0:T(8,128)S(1)}, u32[]{:S(2)}, u32[]{:S(2)}) collective-permute-start(f32[16,1536]{1,0:T(8,128)S(1)} %get-tuple-element.180), channel_id=1, source_target_pairs={{0,32},{32,64},{64,96},{96,128},{128,160},{160,192},{192,224},{224... | collective-permute-start | bytes 294920 | tf_op jit(solution)/shard_map/while/body/eval_jaxpr/ppermute | solution.py:10
  274.4 5.5 %collective-permute-start = (f32[16,1536]{1,0:T(8,128)S(1)}, f32[16,1536]{1,0:T(8,128)S(1)}, u32[]{:S(2)}, u32[]{:S(2)}) collective-permute-start(f32[16,1536]{1,0:T(8,128)S(1)} %get-tuple-element.180), channel_id=1, source_target_pairs={{0,32},{32,64},{64,96},{96,128},{128,160},{160,192},{192,224},{224... | collective-permute-start | bytes 294920 | tf_op jit(solution)/shard_map/while/body/eval_jaxpr/ppermute | solution.py:10
  280.0 1.6 collective-permute-done
  282.5 5.5 %collective-permute-start = (f32[16,1536]{1,0:T(8,128)S(1)}, f32[16,1536]{1,0:T(8,128)S(1)}, u32[]{:S(2)}, u32[]{:S(2)}) collective-permute-start(f32[16,1536]{1,0:T(8,128)S(1)} %get-tuple-element.180), channel_id=1, source_target_pairs={{0,32},{32,64},{64,96},{96,128},{128,160},{160,192},{192,224},{224... | collective-permute-start | bytes 294920 | tf_op jit(solution)/shard_map/while/body/eval_jaxpr/ppermute | solution.py:10
  290.6 5.5 %collective-permute-start = (f32[16,1536]{1,0:T(8,128)S(1)}, f32[16,1536]{1,0:T(8,128)S(1)}, u32[]{:S(2)}, u32[]{:S(2)}) collective-permute-start(f32[16,1536]{1,0:T(8,128)S(1)} %get-tuple-element.180), channel_id=1, source_target_pairs={{0,32},{32,64},{64,96},{96,128},{128,160},{160,192},{192,224},{224... | collective-permute-start | bytes 294920 | tf_op jit(solution)/shard_map/while/body/eval_jaxpr/ppermute | solution.py:10
  296.1 1.6 collective-permute-done
  298.6 5.5 %collective-permute-start = (f32[16,1536]{1,0:T(8,128)S(1)}, f32[16,1536]{1,0:T(8,128)S(1)}, u32[]{:S(2)}, u32[]{:S(2)}) collective-permute-start(f32[16,1536]{1,0:T(8,128)S(1)} %get-tuple-element.180), channel_id=1, source_target_pairs={{0,32},{32,64},{64,96},{96,128},{128,160},{160,192},{192,224},{224... | collective-permute-start | bytes 294920 | tf_op jit(solution)/shard_map/while/body/eval_jaxpr/ppermute | solution.py:10
  306.7 5.5 %collective-permute-start = (f32[16,1536]{1,0:T(8,128)S(1)}, f32[16,1536]{1,0:T(8,128)S(1)}, u32[]{:S(2)}, u32[]{:S(2)}) collective-permute-start(f32[16,1536]{1,0:T(8,128)S(1)} %get-tuple-element.180), channel_id=1, source_target_pairs={{0,32},{32,64},{64,96},{96,128},{128,160},{160,192},{192,224},{224... | collective-permute-start | bytes 294920 | tf_op jit(solution)/shard_map/while/body/eval_jaxpr/ppermute | solution.py:10
  312.2 1.6 collective-permute-done
  314.8 5.5 %collective-permute-start = (f32[16,1536]{1,0:T(8,128)S(1)}, f32[16,1536]{1,0:T(8,128)S(1)}, u32[]{:S(2)}, u32[]{:S(2)}) collective-permute-start(f32[16,1536]{1,0:T(8,128)S(1)} %get-tuple-element.180), channel_id=1, source_target_pairs={{0,32},{32,64},{64,96},{96,128},{128,160},{160,192},{192,224},{224... | collective-permute-start | bytes 294920 | tf_op jit(solution)/shard_map/while/body/eval_jaxpr/ppermute | solution.py:10
  322.8 5.5 %collective-permute-start = (f32[16,1536]{1,0:T(8,128)S(1)}, f32[16,1536]{1,0:T(8,128)S(1)}, u32[]{:S(2)}, u32[]{:S(2)}) collective-permute-start(f32[16,1536]{1,0:T(8,128)S(1)} %get-tuple-element.180), channel_id=1, source_target_pairs={{0,32},{32,64},{64,96},{96,128},{128,160},{160,192},{192,224},{224... | collective-permute-start | bytes 294920 | tf_op jit(solution)/shard_map/while/body/eval_jaxpr/ppermute | solution.py:10
  328.4 1.6 collective-permute-done
  330.1 3.4 copy.32
  333.5 4.6 %reshape.42 = bf16[1536,128]{1,0:T(8,128)(2,1)} reshape(bf16[1536,8,16]{2,1,0:T(8,128)(2,1)} %bitcast.63) | data formatting | bytes 786432
  338.2 71.7 %reduce-scatter.4.cloned.1.call-done = bf16[96,128]{1,0:T(8,128)(2,1)} async-done(((bf16[1536,128]{1,0:T(8,128)(2,1)}), bf16[96,128]{1,0:T(8,128)(2,1)}) %reduce-scatter.4.cloned.1.call-update) | async-done | bytes 24592
  (65 shorter events, 49.3 us)
Async XLA Ops:
  6.5 109.0 %copy-start = (bf16[1,512,1536]{2,1,0:T(8,128)(2,1)S(1)}, bf16[1,512,1536]{2,1,0:T(8,128)(2,1)}, u32[]{:S(2)}) copy-start(bf16[1,512,1536]{2,1,0:T(8,128)(2,1)} %param.11) | copy-start | bytes 4718596
  6.5 109.0 %all-reduce.2.cloned.1.call-start = ((), (), s32[]{:S(2)}) async-start(), calls=%async_computation.3 | async-start | bytes 1572864 | tf_op jit(solution)/shard_map/psum | solution.py:50
  122.1 6.7 %copy-start.2 = (f32[8,1,16]{2,1,0:T(1,128)S(1)}, f32[8,1,16]{2,1,0:T(1,128)}, u32[]{:S(2)}) copy-start(f32[8,1,16]{2,1,0:T(1,128)} %param.13) | copy-start | bytes 1540
  122.1 38.6 %all-to-all-start.1 = ((bf16[8,8,6,1536]{3,1,2,0:T(8,128)(2,1)}), bf16[8,8,6,1536]{3,1,2,0:T(8,128)(2,1)S(1)}, u32[]{:S(2)}, u32[]{:S(2)}) async-start(bf16[8,8,6,1536]{3,1,2,0:T(8,128)(2,1)} %copy.27), calls=%async_computation.1 | async-start | bytes 2359296 | tf_op jit(solution)/shard_map/all_to_all | solution.py:54
  128.8 281.0 %reduce-scatter.4.cloned.1.call-start = ((), (), s32[]{:S(2)}) async-start(), calls=%async_computation.4 | async-start | bytes 417792
  163.4 166.6 %copy-start.1 = (bf16[8,1,16,1536]{3,2,1,0:T(8,128)(2,1)S(1)}, bf16[8,1,16,1536]{3,2,1,0:T(8,128)(2,1)}, u32[]{:S(2)}) copy-start(bf16[8,1,16,1536]{3,2,1,0:T(8,128)(2,1)} %param.8) | copy-start | bytes 1179652
  164.4 5.4 %collective-permute-start = (f32[16,1536]{1,0:T(8,128)S(1)}, f32[16,1536]{1,0:T(8,128)S(1)}, u32[]{:S(2)}, u32[]{:S(2)}) collective-permute-start(f32[16,1536]{1,0:T(8,128)S(1)} %get-tuple-element.180), channel_id=1, source_target_pairs={{0,32},{32,64},{64,96},{96,128},{128,160},{160,192},{192,224},{224... | collective-permute-start | bytes 294920 | tf_op jit(solution)/shard_map/while/body/eval_jaxpr/ppermute | solution.py:10
  170.7 5.9 %collective-permute-start = (f32[16,1536]{1,0:T(8,128)S(1)}, f32[16,1536]{1,0:T(8,128)S(1)}, u32[]{:S(2)}, u32[]{:S(2)}) collective-permute-start(f32[16,1536]{1,0:T(8,128)S(1)} %get-tuple-element.180), channel_id=1, source_target_pairs={{0,32},{32,64},{64,96},{96,128},{128,160},{160,192},{192,224},{224... | collective-permute-start | bytes 294920 | tf_op jit(solution)/shard_map/while/body/eval_jaxpr/ppermute | solution.py:10
  177.6 5.9 %collective-permute-start = (f32[16,1536]{1,0:T(8,128)S(1)}, f32[16,1536]{1,0:T(8,128)S(1)}, u32[]{:S(2)}, u32[]{:S(2)}) collective-permute-start(f32[16,1536]{1,0:T(8,128)S(1)} %get-tuple-element.180), channel_id=1, source_target_pairs={{0,32},{32,64},{64,96},{96,128},{128,160},{160,192},{192,224},{224... | collective-permute-start | bytes 294920 | tf_op jit(solution)/shard_map/while/body/eval_jaxpr/ppermute | solution.py:10
  184.5 5.9 %collective-permute-start = (f32[16,1536]{1,0:T(8,128)S(1)}, f32[16,1536]{1,0:T(8,128)S(1)}, u32[]{:S(2)}, u32[]{:S(2)}) collective-permute-start(f32[16,1536]{1,0:T(8,128)S(1)} %get-tuple-element.180), channel_id=1, source_target_pairs={{0,32},{32,64},{64,96},{96,128},{128,160},{160,192},{192,224},{224... | collective-permute-start | bytes 294920 | tf_op jit(solution)/shard_map/while/body/eval_jaxpr/ppermute | solution.py:10
  191.3 5.9 %collective-permute-start = (f32[16,1536]{1,0:T(8,128)S(1)}, f32[16,1536]{1,0:T(8,128)S(1)}, u32[]{:S(2)}, u32[]{:S(2)}) collective-permute-start(f32[16,1536]{1,0:T(8,128)S(1)} %get-tuple-element.180), channel_id=1, source_target_pairs={{0,32},{32,64},{64,96},{96,128},{128,160},{160,192},{192,224},{224... | collective-permute-start | bytes 294920 | tf_op jit(solution)/shard_map/while/body/eval_jaxpr/ppermute | solution.py:10
  198.2 5.9 %collective-permute-start = (f32[16,1536]{1,0:T(8,128)S(1)}, f32[16,1536]{1,0:T(8,128)S(1)}, u32[]{:S(2)}, u32[]{:S(2)}) collective-permute-start(f32[16,1536]{1,0:T(8,128)S(1)} %get-tuple-element.180), channel_id=1, source_target_pairs={{0,32},{32,64},{64,96},{96,128},{128,160},{160,192},{192,224},{224... | collective-permute-start | bytes 294920 | tf_op jit(solution)/shard_map/while/body/eval_jaxpr/ppermute | solution.py:10
  205.0 5.9 %collective-permute-start = (f32[16,1536]{1,0:T(8,128)S(1)}, f32[16,1536]{1,0:T(8,128)S(1)}, u32[]{:S(2)}, u32[]{:S(2)}) collective-permute-start(f32[16,1536]{1,0:T(8,128)S(1)} %get-tuple-element.180), channel_id=1, source_target_pairs={{0,32},{32,64},{64,96},{96,128},{128,160},{160,192},{192,224},{224... | collective-permute-start | bytes 294920 | tf_op jit(solution)/shard_map/while/body/eval_jaxpr/ppermute | solution.py:10
  211.9 5.9 %collective-permute-start = (f32[16,1536]{1,0:T(8,128)S(1)}, f32[16,1536]{1,0:T(8,128)S(1)}, u32[]{:S(2)}, u32[]{:S(2)}) collective-permute-start(f32[16,1536]{1,0:T(8,128)S(1)} %get-tuple-element.180), channel_id=1, source_target_pairs={{0,32},{32,64},{64,96},{96,128},{128,160},{160,192},{192,224},{224... | collective-permute-start | bytes 294920 | tf_op jit(solution)/shard_map/while/body/eval_jaxpr/ppermute | solution.py:10
  218.7 5.9 %collective-permute-start = (f32[16,1536]{1,0:T(8,128)S(1)}, f32[16,1536]{1,0:T(8,128)S(1)}, u32[]{:S(2)}, u32[]{:S(2)}) collective-permute-start(f32[16,1536]{1,0:T(8,128)S(1)} %get-tuple-element.180), channel_id=1, source_target_pairs={{0,32},{32,64},{64,96},{96,128},{128,160},{160,192},{192,224},{224... | collective-permute-start | bytes 294920 | tf_op jit(solution)/shard_map/while/body/eval_jaxpr/ppermute | solution.py:10
  225.6 5.9 %collective-permute-start = (f32[16,1536]{1,0:T(8,128)S(1)}, f32[16,1536]{1,0:T(8,128)S(1)}, u32[]{:S(2)}, u32[]{:S(2)}) collective-permute-start(f32[16,1536]{1,0:T(8,128)S(1)} %get-tuple-element.180), channel_id=1, source_target_pairs={{0,32},{32,64},{64,96},{96,128},{128,160},{160,192},{192,224},{224... | collective-permute-start | bytes 294920 | tf_op jit(solution)/shard_map/while/body/eval_jaxpr/ppermute | solution.py:10
  232.4 5.9 %collective-permute-start = (f32[16,1536]{1,0:T(8,128)S(1)}, f32[16,1536]{1,0:T(8,128)S(1)}, u32[]{:S(2)}, u32[]{:S(2)}) collective-permute-start(f32[16,1536]{1,0:T(8,128)S(1)} %get-tuple-element.180), channel_id=1, source_target_pairs={{0,32},{32,64},{64,96},{96,128},{128,160},{160,192},{192,224},{224... | collective-permute-start | bytes 294920 | tf_op jit(solution)/shard_map/while/body/eval_jaxpr/ppermute | solution.py:10
  239.3 5.9 %collective-permute-start = (f32[16,1536]{1,0:T(8,128)S(1)}, f32[16,1536]{1,0:T(8,128)S(1)}, u32[]{:S(2)}, u32[]{:S(2)}) collective-permute-start(f32[16,1536]{1,0:T(8,128)S(1)} %get-tuple-element.180), channel_id=1, source_target_pairs={{0,32},{32,64},{64,96},{96,128},{128,160},{160,192},{192,224},{224... | collective-permute-start | bytes 294920 | tf_op jit(solution)/shard_map/while/body/eval_jaxpr/ppermute | solution.py:10
  246.1 5.9 %collective-permute-start = (f32[16,1536]{1,0:T(8,128)S(1)}, f32[16,1536]{1,0:T(8,128)S(1)}, u32[]{:S(2)}, u32[]{:S(2)}) collective-permute-start(f32[16,1536]{1,0:T(8,128)S(1)} %get-tuple-element.180), channel_id=1, source_target_pairs={{0,32},{32,64},{64,96},{96,128},{128,160},{160,192},{192,224},{224... | collective-permute-start | bytes 294920 | tf_op jit(solution)/shard_map/while/body/eval_jaxpr/ppermute | solution.py:10
  253.0 5.9 %collective-permute-start = (f32[16,1536]{1,0:T(8,128)S(1)}, f32[16,1536]{1,0:T(8,128)S(1)}, u32[]{:S(2)}, u32[]{:S(2)}) collective-permute-start(f32[16,1536]{1,0:T(8,128)S(1)} %get-tuple-element.180), channel_id=1, source_target_pairs={{0,32},{32,64},{64,96},{96,128},{128,160},{160,192},{192,224},{224... | collective-permute-start | bytes 294920 | tf_op jit(solution)/shard_map/while/body/eval_jaxpr/ppermute | solution.py:10
  259.8 5.9 %collective-permute-start = (f32[16,1536]{1,0:T(8,128)S(1)}, f32[16,1536]{1,0:T(8,128)S(1)}, u32[]{:S(2)}, u32[]{:S(2)}) collective-permute-start(f32[16,1536]{1,0:T(8,128)S(1)} %get-tuple-element.180), channel_id=1, source_target_pairs={{0,32},{32,64},{64,96},{96,128},{128,160},{160,192},{192,224},{224... | collective-permute-start | bytes 294920 | tf_op jit(solution)/shard_map/while/body/eval_jaxpr/ppermute | solution.py:10
  266.7 6.8 %collective-permute-start = (f32[16,1536]{1,0:T(8,128)S(1)}, f32[16,1536]{1,0:T(8,128)S(1)}, u32[]{:S(2)}, u32[]{:S(2)}) collective-permute-start(f32[16,1536]{1,0:T(8,128)S(1)} %get-tuple-element.180), channel_id=1, source_target_pairs={{0,32},{32,64},{64,96},{96,128},{128,160},{160,192},{192,224},{224... | collective-permute-start | bytes 294920 | tf_op jit(solution)/shard_map/while/body/eval_jaxpr/ppermute | solution.py:10
  274.4 7.1 %collective-permute-start = (f32[16,1536]{1,0:T(8,128)S(1)}, f32[16,1536]{1,0:T(8,128)S(1)}, u32[]{:S(2)}, u32[]{:S(2)}) collective-permute-start(f32[16,1536]{1,0:T(8,128)S(1)} %get-tuple-element.180), channel_id=1, source_target_pairs={{0,32},{32,64},{64,96},{96,128},{128,160},{160,192},{192,224},{224... | collective-permute-start | bytes 294920 | tf_op jit(solution)/shard_map/while/body/eval_jaxpr/ppermute | solution.py:10
  282.5 7.1 %collective-permute-start = (f32[16,1536]{1,0:T(8,128)S(1)}, f32[16,1536]{1,0:T(8,128)S(1)}, u32[]{:S(2)}, u32[]{:S(2)}) collective-permute-start(f32[16,1536]{1,0:T(8,128)S(1)} %get-tuple-element.180), channel_id=1, source_target_pairs={{0,32},{32,64},{64,96},{96,128},{128,160},{160,192},{192,224},{224... | collective-permute-start | bytes 294920 | tf_op jit(solution)/shard_map/while/body/eval_jaxpr/ppermute | solution.py:10
  290.6 7.1 %collective-permute-start = (f32[16,1536]{1,0:T(8,128)S(1)}, f32[16,1536]{1,0:T(8,128)S(1)}, u32[]{:S(2)}, u32[]{:S(2)}) collective-permute-start(f32[16,1536]{1,0:T(8,128)S(1)} %get-tuple-element.180), channel_id=1, source_target_pairs={{0,32},{32,64},{64,96},{96,128},{128,160},{160,192},{192,224},{224... | collective-permute-start | bytes 294920 | tf_op jit(solution)/shard_map/while/body/eval_jaxpr/ppermute | solution.py:10
  298.6 7.1 %collective-permute-start = (f32[16,1536]{1,0:T(8,128)S(1)}, f32[16,1536]{1,0:T(8,128)S(1)}, u32[]{:S(2)}, u32[]{:S(2)}) collective-permute-start(f32[16,1536]{1,0:T(8,128)S(1)} %get-tuple-element.180), channel_id=1, source_target_pairs={{0,32},{32,64},{64,96},{96,128},{128,160},{160,192},{192,224},{224... | collective-permute-start | bytes 294920 | tf_op jit(solution)/shard_map/while/body/eval_jaxpr/ppermute | solution.py:10
  306.7 7.1 %collective-permute-start = (f32[16,1536]{1,0:T(8,128)S(1)}, f32[16,1536]{1,0:T(8,128)S(1)}, u32[]{:S(2)}, u32[]{:S(2)}) collective-permute-start(f32[16,1536]{1,0:T(8,128)S(1)} %get-tuple-element.180), channel_id=1, source_target_pairs={{0,32},{32,64},{64,96},{96,128},{128,160},{160,192},{192,224},{224... | collective-permute-start | bytes 294920 | tf_op jit(solution)/shard_map/while/body/eval_jaxpr/ppermute | solution.py:10
  314.8 7.1 %collective-permute-start = (f32[16,1536]{1,0:T(8,128)S(1)}, f32[16,1536]{1,0:T(8,128)S(1)}, u32[]{:S(2)}, u32[]{:S(2)}) collective-permute-start(f32[16,1536]{1,0:T(8,128)S(1)} %get-tuple-element.180), channel_id=1, source_target_pairs={{0,32},{32,64},{64,96},{96,128},{128,160},{160,192},{192,224},{224... | collective-permute-start | bytes 294920 | tf_op jit(solution)/shard_map/while/body/eval_jaxpr/ppermute | solution.py:10
  322.8 7.1 %collective-permute-start = (f32[16,1536]{1,0:T(8,128)S(1)}, f32[16,1536]{1,0:T(8,128)S(1)}, u32[]{:S(2)}, u32[]{:S(2)}) collective-permute-start(f32[16,1536]{1,0:T(8,128)S(1)} %get-tuple-element.180), channel_id=1, source_target_pairs={{0,32},{32,64},{64,96},{96,128},{128,160},{160,192},{192,224},{224... | collective-permute-start | bytes 294920 | tf_op jit(solution)/shard_map/while/body/eval_jaxpr/ppermute | solution.py:10
Sparse Core Ops, SparseCore 0:
  61.2 54.3 all-reduce.1
  338.3 71.5 reduce-scatter.3
where the time goes:
time: 422 us; the launch traced here: 418 us
  waiting for transfers between devices  195 us (46%)
  starting transfers between devices  115 us (27%)
  blocking collectives  43.9 us (10%)
  other arithmetic  23.7 us (6%)
  local copies, waits for them, and re-layouts  16.5 us (4%)
  between operations  13.5 us (3%)
  matrix products  10.5 us (2%)
    ppermute x23, starting transfers between devices, shifted_2(): lax.ppermute(value, axis, [(source, source + steps) for source in range(i...  108 us
    unnamed x3, waiting for transfers between devices  71.7 us
    psum x1, waiting for transfers between devices, on_device(): gate_total = lax.psum(partial_value, 'dp')  54.5 us
    ppermute x23, waiting for transfers between devices, shifted_2(): lax.ppermute(value, axis, [(source, source + steps) for source in range(i...  37.1 us
    all_to_all x1, blocking collectives, on_device(): lax.all_to_all(outgoing, 'expert', split_axis=0, concat_axis=0, tiled=True)  34.6 us
    all_to_all x1, waiting for transfers between devices, on_device(): lax.all_to_all(expert_out, 'expert', split_axis=0, concat_axis=0, tiled=T...  31.8 us
    select_n x23, other arithmetic, advance(): jnp.where(is_live & (my_segment == segments - 1), updated, finished)  21.1 us
    unnamed x10, local copies, waits for them, and re-layouts  9.74 us
  transfers between devices with their start and end apart: 26, of which 26 were waited for; matrix products, arithmetic and copies ran while one was open for 0% of the time, Pallas kernels for 0%

commit v1 on v0

v1 whole, which is shorter than its diff:
```python
import jax
import jax.numpy as jnp
from jax import lax
from jax.experimental import pallas as pl
from jax.experimental.pallas import tpu as pltpu
from jax.sharding import PartitionSpec as P

MESH = pl.DeviceIdType.MESH
OFFSETS = (0, 1, -1, 2, -2, 3, -3, 4)
GROUPS = 2
SLOTS = 8
PER = 4
CAP = 6
F32 = jnp.float32
BF16 = jnp.bfloat16


def layer_kernel(
    tok_ref, gain_ref, meta_ref, up_hbm, down_hbm, out_ref,
    wu, wd, pk, xg, xn, rs, rr, hb, cs, cr, zs, zr, ys, ret, pwh, pwl,
    w_sem, a_s, a_r, b_s, b_r, c_s, c_r, d_s, d_r, e_s, e_r, f_s, f_r, g_s, g_r,
):
    p = lax.axis_index("pipe")
    y = lax.axis_index("expert")
    x = lax.axis_index("dp")
    n_y = lax.axis_size("expert")
    n_x = lax.axis_size("dp")
    n_z = lax.axis_size("pipe") // 2
    z = p // 2
    c = p % 2
    partner = 2 * z + 1 - c
    n_tok, width = tok_ref.shape
    half = width // 2
    rows = pk.shape[1]
    units = wu.shape[1]
    feats = width // (2 * n_z)
    lane_group = PER * feats

    def dev_y(offset):
        return (p, lax.rem(y + offset + n_y, n_y), x)

    def dev_x(j):
        return (p, y, lax.rem(x + j, n_x))

    def dev_z(j):
        return (2 * lax.rem(z + j, n_z) + c, y, x)

    def remote(src, dst, s, r, dev):
        return pltpu.make_async_remote_copy(
            src_ref=src, dst_ref=dst, send_sem=s, recv_sem=r, device_id=dev, device_id_type=MESH
        )

    weight_copies = [pltpu.make_async_copy(up_hbm, wu, w_sem.at[0])]
    for part in range(wd.shape[0]):
        weight_copies.append(
            pltpu.make_async_copy(
                down_hbm.at[:, pl.ds(part * lane_group, lane_group)], wd.at[part], w_sem.at[1 + part]
            )
        )
    for copy in weight_copies:
        copy.start()

    barrier = pltpu.get_barrier_semaphore()
    peers = [dev_y(o) for o in OFFSETS[1:]] + [dev_x(j) for j in range(1, 4)]
    peers += [dev_z(j) for j in range(1, 8)] + [(partner, y, x)]
    for dev in peers:
        pl.semaphore_signal(barrier, inc=1, device_id=dev, device_id_type=MESH)

    sub = lax.broadcasted_iota(jnp.int32, (SLOTS, n_tok), 0)
    lane = lax.broadcasted_iota(jnp.int32, (SLOTS, n_tok), 1)
    offset = jnp.zeros_like(sub)
    for k in range(SLOTS):
        offset = jnp.where(sub == k, OFFSETS[k], offset)
    expert_of = y - offset
    expert_of = jnp.where(expert_of < 0, expert_of + n_y, expert_of)
    expert_of = jnp.where(expert_of >= n_y, expert_of - n_y, expert_of).astype(F32)
    first = meta_ref[0:1, :] == expert_of
    second = meta_ref[1:2, :] == expert_of
    share = 1.0 / (1.0 + jnp.exp(-meta_ref[2:3, :]))
    weight = jnp.where(first, share, 0.0) + jnp.where(second, 1.0 - share, 0.0)
    member = first | second
    before = lax.broadcasted_iota(jnp.int32, (n_tok, n_tok), 0)
    token = lax.broadcasted_iota(jnp.int32, (n_tok, n_tok), 1)
    block_of = (token // 16) == (before // 16)
    earlier = jnp.where(block_of & (before < token), 1.0, 0.0).astype(BF16)
    rank = jnp.dot(jnp.where(member, 1.0, 0.0).astype(BF16), earlier, preferred_element_type=F32)
    code = jnp.where(member, rank + ((lane // 16) * CAP).astype(F32), -1.0)
    row_id = lax.broadcasted_iota(jnp.int32, (rows, n_tok), 0).astype(F32)
    lo_half = pl.multiple_of(c * half, 128)
    own_half = tok_ref[:, pl.ds(lo_half, half)]
    for k in range(SLOTS):
        hit = code[k : k + 1, :] == row_id
        pick = jnp.where(hit, 1.0, 0.0).astype(BF16)
        if k == 0:
            both = jnp.dot(pick, tok_ref[...], preferred_element_type=F32).astype(BF16)
            xg[0, 0] = both[:, :half]
            xg[1, 0] = both[:, half:]
        else:
            pk[k] = jnp.dot(pick, own_half, preferred_element_type=F32).astype(BF16)

    pl.semaphore_wait(barrier, len(peers))

    a_copies = [None]
    for k in range(1, SLOTS):
        copy = remote(pk.at[k], xg.at[c, k], a_s.at[k], a_r.at[k], dev_y(-OFFSETS[k]))
        copy.start()
        a_copies.append(copy)

    for k in range(SLOTS):
        hit = code[k : k + 1, :] == row_id
        placed = jnp.where(hit, weight[k : k + 1, :], 0.0)
        high = placed.astype(BF16)
        pwh[pl.ds(k * rows, rows), :] = high
        pwl[pl.ds(k * rows, rows), :] = (placed - high.astype(F32)).astype(BF16)

    b_copies = {}
    c_copies, d_copies, e_copies, f_copies, g_copies = {}, {}, {}, {}, {}

    def prepare(g, q, k, h, total):
        lo = pl.multiple_of(h * half, 128) if not isinstance(h, int) else h * half
        block = xg[h, k].astype(F32)
        total = total + jnp.sum(block * block, axis=-1, keepdims=True)
        xn[g, pl.ds(q * rows, rows), pl.ds(lo, half)] = (block * gain_ref[:, pl.ds(lo, half)]).astype(BF16)
        return total

    def stage_a(g):
        totals = []
        for q in range(PER):
            k = g * PER + q
            total = jnp.zeros((rows, 1), F32)
            if k > 0:
                a_copies[k].wait_recv()
                b_copies[k] = remote(xg.at[c, k], xg.at[c, k], b_s.at[k], b_r.at[k], (partner, y, x))
                b_copies[k].start()
                total = prepare(g, q, k, c, total)
            else:
                total = prepare(g, q, k, 0, total)
                total = prepare(g, q, k, 1, total)
            totals.append(total)
        for q in range(PER):
            k = g * PER + q
            if k > 0:
                b_copies[k].wait_recv()
                totals[q] = prepare(g, q, k, 1 - c, totals[q])
        if g == 0:
            weight_copies[0].wait()
        gate = jnp.dot(xn[g], wu[...], preferred_element_type=F32)
        lanes = lax.broadcasted_iota(jnp.int32, (rows, 128), 1)
        for q in range(PER):
            rs[g, q, :, pl.ds(0, units)] = gate[q * rows : (q + 1) * rows].astype(BF16)
            square = jnp.broadcast_to(totals[q], (rows, 128))
            high = square.astype(BF16).astype(F32)
            rs[g, q, :, pl.ds(units, 128)] = jnp.where(lanes < 64, high, square - high).astype(BF16)
        for j in range(1, 4):
            copy = remote(rs.at[g, lax.rem(x + j, n_x)], rr.at[g, j], c_s.at[g, j], c_r.at[g, j], dev_x(j))
            copy.start()
            c_copies[g, j] = copy

    def stage_b(g):
        total = rs[g, x].astype(F32)
        for j in range(1, 4):
            c_copies[g, j].wait_recv()
            total = total + rr[g, j].astype(F32)
        square = total[:, units : units + 1] + total[:, units + 64 : units + 65]
        scale = lax.rsqrt(square / (width * n_x) + 1e-05)
        gate = total[:, :units] * scale
        hb[g, x] = (gate / (1.0 + jnp.exp(-gate))).astype(BF16)
        for j in range(1, 4):
            copy = remote(hb.at[g, x], hb.at[g, x], d_s.at[g, j], d_r.at[g, j], dev_x(j))
            copy.start()
            d_copies[g, j] = copy

    def stage_c(g):
        for j in range(1, 4):
            d_copies[g, j].wait_recv()
        hidden = hb[g].reshape(PER * rows, units)
        if g == 0:
            for copy in weight_copies[1:]:
                copy.wait()
        lanes = lax.broadcasted_iota(jnp.int32, (rows, lane_group), 1)
        for part in range(wd.shape[0]):
            outs = jnp.dot(hidden, wd[part], preferred_element_type=F32)
            for r in range(PER):
                packed = None
                for q in range(PER):
                    piece = outs[q * rows : (q + 1) * rows]
                    shift = ((q - r) % PER) * feats
                    moved = piece if shift == 0 else pltpu.roll(piece, shift, 1)
                    packed = moved if packed is None else jnp.where(lanes >= q * feats, moved, packed)
                cs[g, r % 2, 2 * part + r // 2] = packed.astype(BF16)
            copy = remote(
                cs.at[g, 1 - c, pl.ds(2 * part, 2)], cr.at[g, pl.ds(2 * part, 2)],
                e_s.at[g, part], e_r.at[g, part], (partner, y, x),
            )
            copy.start()
            e_copies[g, part] = copy

    def stage_d(g):
        for part in range(wd.shape[0]):
            e_copies[g, part].wait_recv()
        for j in (4, 3, 5, 2, 6, 1, 7):
            to = lax.rem(z + j, n_z)
            zs[g, j] = (cs[g, c, to].astype(F32) + cr[g, to].astype(F32)).astype(BF16)
            copy = remote(zs.at[g, j], zr.at[g, j], f_s.at[g, j], f_r.at[g, j], dev_z(j))
            copy.start()
            f_copies[g, j] = copy

    def stage_e(g):
        total = cs[g, c, z].astype(F32) + cr[g, z].astype(F32)
        for j in (1, 7, 2, 6, 3, 5, 4):
            f_copies[g, j].wait_recv()
            total = total + zr[g, j].astype(F32)
        for q in reversed(range(PER)):
            k = g * PER + q
            moved = total if q == 0 else pltpu.roll(total, lane_group - q * feats, 1)
            block = moved[:, :128].astype(BF16)
            if k == 0:
                ret[0] = block
            else:
                ys[k] = block
                copy = remote(ys.at[k], ret.at[k], g_s.at[k], g_r.at[k], dev_y(OFFSETS[k]))
                copy.start()
                g_copies[k] = copy

    stage_a(0)
    stage_b(0)
    stage_c(0)
    stage_d(0)
    stage_a(1)
    stage_b(1)
    stage_c(1)
    stage_d(1)
    stage_e(0)
    stage_e(1)
    for k in range(1, SLOTS):
        g_copies[k].wait_recv()
    back = ret[...].reshape(SLOTS * rows, 128)
    dims = (((0,), (0,)), ((), ()))
    moe = lax.dot_general(pwh[...], back, dims, preferred_element_type=F32)
    moe = moe + lax.dot_general(pwl[...], back, dims, preferred_element_type=F32)
    out_ref[...] = moe
    for copy in a_copies[1:]:
        copy.wait_send()
    for group in (b_copies, c_copies, d_copies, e_copies, f_copies, g_copies):
        for copy in group.values():
            copy.wait_send()


def on_device(tokens, norm_gain, up_w, down_w, expert_ids, gate_gap):
    micro, _, row_count, width = tokens.shape
    n_tok = micro * row_count
    rows = micro * CAP
    units = up_w.shape[2]
    pipe = lax.axis_size("pipe")
    n_z = pipe // 2
    feats = width // pipe
    lane_group = PER * feats
    parts = width // lane_group
    flat = tokens.reshape(n_tok, width)
    ids = expert_ids[:, 0].reshape(n_tok, 2).T.astype(F32)
    gap = gate_gap[:, 0].reshape(1, n_tok)
    meta = jnp.concatenate([ids, gap], axis=0)
    vmem = pl.BlockSpec(memory_space=pltpu.VMEM)
    hbm = pl.BlockSpec(memory_space=pl.ANY)
    dma = pltpu.SemaphoreType.DMA
    moe = pl.pallas_call(
        layer_kernel,
        out_shape=jax.ShapeDtypeStruct((n_tok, 128), F32),
        in_specs=[vmem, vmem, vmem, hbm, hbm],
        out_specs=vmem,
        scratch_shapes=[
            pltpu.VMEM((width, units), BF16),
            pltpu.VMEM((parts, units, lane_group), BF16),
            pltpu.VMEM((SLOTS, rows, width // 2), BF16),
            pltpu.VMEM((2, SLOTS, rows, width // 2), BF16),
            pltpu.VMEM((GROUPS, PER * rows, width), BF16),
            pltpu.VMEM((GROUPS, PER, rows, units + 128), BF16),
            pltpu.VMEM((GROUPS, 4, rows, units + 128), BF16),
            pltpu.VMEM((GROUPS, PER, rows, units), BF16),
            pltpu.VMEM((GROUPS, 2, n_z, rows, lane_group), BF16),
            pltpu.VMEM((GROUPS, n_z, rows, lane_group), BF16),
            pltpu.VMEM((GROUPS, n_z, rows, lane_group), BF16),
            pltpu.VMEM((GROUPS, n_z, rows, lane_group), BF16),
            pltpu.VMEM((SLOTS, rows, 128), BF16),
            pltpu.VMEM((SLOTS, rows, 128), BF16),
            pltpu.VMEM((SLOTS * rows, n_tok), BF16),
            pltpu.VMEM((SLOTS * rows, n_tok), BF16),
            dma((1 + parts,)),
            dma((SLOTS,)), dma((SLOTS,)),
            dma((SLOTS,)), dma((SLOTS,)),
            dma((GROUPS, 4)), dma((GROUPS, 4)),
            dma((GROUPS, 4)), dma((GROUPS, 4)),
            dma((GROUPS, parts)), dma((GROUPS, parts)),
            dma((GROUPS, n_z)), dma((GROUPS, n_z)),
            dma((SLOTS,)), dma((SLOTS,)),
        ],
        compiler_params=pltpu.CompilerParams(
            collective_id=0, has_side_effects=True, vmem_limit_bytes=56 * 1024 * 1024
        ),
        name="expert_layer",
    )(flat, norm_gain.reshape(1, width), meta, up_w[0], down_w[0])
    start = lax.axis_index("pipe") * feats
    own = lax.dynamic_slice_in_dim(flat, start, feats, axis=1).astype(F32)
    result = (own + moe[:, :feats]).astype(BF16)
    return result.reshape(micro, 1, row_count, feats)


def solution(mesh):
    return jax.shard_map(
        on_device,
        mesh=mesh,
        in_specs=(
            P(None, "expert", None, "dp"),
            P("dp"),
            P("expert", "dp", "pipe"),
            P("expert", "pipe", "dp"),
            P(None, "expert", None, None),
            P(None, "expert", None),
        ),
        out_specs=P(None, "expert", None, ("dp", "pipe")),
        check_vma=False,
    )
```

time: 422 us -> 76.3 us (0.18)
  waiting for transfers between devices: 195 us -> 0 us
  starting transfers between devices: 115 us -> 0 us
  Pallas kernels: 0 us -> 69.8 us
  blocking collectives: 43.9 us -> 0 us
  other arithmetic: 23.7 us -> 4.2 us
  local copies, waits for them, and re-layouts: 16.5 us -> 1.97 us
  between operations: 13.5 us -> 0.02 us
  matrix products: 10.5 us -> 0 us
    ppermute x23 -> x0, starting transfers between devices: 108 us -> none  [shifted_2(): lax.ppermute(value, axis, [(source, source + steps) for source in range(i...]
    unnamed x3 -> x0, waiting for transfers between devices: 71.7 us -> none
    pallas_call x0 -> x1, Pallas kernels: none -> 69.8 us  [on_device(): pl.pallas_call(layer_kernel, out_shape=jax.ShapeDtypeStruct((n_tok, 128),...]
    psum x1 -> x0, waiting for transfers between devices: 54.5 us -> none  [on_device(): gate_total = lax.psum(partial_value, 'dp')]
    ppermute x23 -> x0, waiting for transfers between devices: 37.1 us -> none  [shifted_2(): lax.ppermute(value, axis, [(source, source + steps) for source in range(i...]
    all_to_all x1 -> x0, blocking collectives: 34.6 us -> none  [on_device(): lax.all_to_all(outgoing, 'expert', split_axis=0, concat_axis=0, tiled=True)]
    all_to_all x1 -> x0, waiting for transfers between devices: 31.8 us -> none  [on_device(): lax.all_to_all(expert_out, 'expert', split_axis=0, concat_axis=0, tiled=T...]
    select_n x23 -> x0, other arithmetic: 21.1 us -> none  [advance(): jnp.where(is_live & (my_segment == segments - 1), updated, finished)]
  transfers between devices with their start and end apart: 26 -> 0, of which waited for: 26 -> 0; matrix products, arithmetic and copies ran while one was open for 0% -> 0% of each run, Pallas kernels for 0% -> 0%
where the time goes in v1:
time: 76.3 us; the launch traced here: 76 us
  Pallas kernels  69.8 us (91%)
  other arithmetic  4.2 us (6%)
  local copies, waits for them, and re-layouts  1.97 us (3%)
    pallas_call x1, Pallas kernels, on_device(): pl.pallas_call(layer_kernel, out_shape=jax.ShapeDtypeStruct((n_tok, 128),...  69.8 us
    convert_element_type x1, other arithmetic, on_device(): result = (own + moe[:, :feats]).astype(BF16)  1.57 us

profile of v1, /device:TPU:1, one launch (start us, length us, event | category | flops | bytes accessed | tf_op | source)
XLA Modules:
  0.0 76.0 jit_solution(1708989993881222899)
XLA Ops:
  0.0 0.5 broadcast.3
  0.5 1.3 %reduce.3 = f32[8,16]{1,0:T(8,128)S(1)} reduce(f32[8,1,16]{2,1,0:T(1,128)} %param.11, f32[]{:T(128)} %broadcast.3), dimensions={1}, to_apply=%param.11.reduce_sub_computation.3 | reduce | bytes 1028 | tf_op args[5]
  1.9 0.1 reshape_squeeze.4
  1.9 1.3 %reshape.11.gain_ref = f32[1,1536]{1,0:T(1,128)} reshape(f32[1536]{0:T(1024)} %param.7) | data formatting | bytes 12288 | tf_op jit(solution)/shard_map/reshape | solution.py:301
  3.2 0.7 convert_element_type.16
  3.9 0.1 convert_element_type.17
  4.0 0.6 pad_maximum_fusion.meta_ref
  4.6 69.8 %expert_layer.1 = f32[128,128]{1,0:T(8,128)} custom-call(bf16[128,1536]{1,0:T(8,128)(2,1)} %bitcast.13, f32[1,1536]{1,0:T(1,128)} %reshape.11.gain_ref, f32[3,128]{1,0:T(4,128)} %pad_maximum_fusion.meta_ref, bf16[1536,512]{1,0:T(8,128)(2,1)} %bitcast.11, bf16[512,1536]{1,0:T(8,128)(2,1)} %bitcast.12), custom_call_target="tpu_custom_call" | custom-call | tf_op jit(solution)/shard_map/expert_layer/pallas_call | solution.py:266
  74.4 1.6 %add_convert_fusion = bf16[128,96]{1,0:T(8,128)(2,1)} fusion(f32[128,128]{1,0:T(8,128)} %expert_layer.1, bf16[128,1536]{1,0:T(8,128)(2,1)} %bitcast.14, s32[]{:T(128)S(6)} %select_n.3), kind=kLoop, calls=%fused_computation | loop fusion | flops 36864 | bytes 98308 | tf_op jit(solution)/shard_map/convert_element_type | solution.py:304
  (1 shorter events, 0.0 us)

commit v2 on v1

--- a/solution.py
+++ b/solution.py
@@ -16,8 +16,8 @@
 
 
 def layer_kernel(
-    tok_ref, gain_ref, meta_ref, up_hbm, down_hbm, out_ref,
-    wu, wd, pk, xg, xn, rs, rr, hb, cs, cr, zs, zr, ys, ret, pwh, pwl,
+    tok_hbm, gain_ref, ids_ref, gap_ref, up_hbm, down_hbm, out_ref,
+    tok_ref, wu, wd, pk, xg, xn, rs, rr, hb, cs, cr, zs, zr, ys, ret, pwh, pwl,
     w_sem, a_s, a_r, b_s, b_r, c_s, c_r, d_s, d_r, e_s, e_r, f_s, f_r, g_s, g_r,
 ):
     p = lax.axis_index("pipe")
@@ -31,7 +31,8 @@
     partner = 2 * z + 1 - c
     n_tok, width = tok_ref.shape
     half = width // 2
-    rows = pk.shape[1]
+    rows = n_tok // 16 * CAP
+    row_half, lane_half = pk.shape[2:]
     units = wu.shape[1]
     feats = width // (2 * n_z)
     lane_group = PER * feats
@@ -49,22 +50,24 @@
         return pltpu.make_async_remote_copy(
             src_ref=src, dst_ref=dst, send_sem=s, recv_sem=r, device_id=dev, device_id_type=MESH
         )
-
-    weight_copies = [pltpu.make_async_copy(up_hbm, wu, w_sem.at[0])]
-    for part in range(wd.shape[0]):
-        weight_copies.append(
-            pltpu.make_async_copy(
-                down_hbm.at[:, pl.ds(part * lane_group, lane_group)], wd.at[part], w_sem.at[1 + part]
-            )
-        )
-    for copy in weight_copies:
-        copy.start()
 
     barrier = pltpu.get_barrier_semaphore()
     peers = [dev_y(o) for o in OFFSETS[1:]] + [dev_x(j) for j in range(1, 4)]
     peers += [dev_z(j) for j in range(1, 8)] + [(partner, y, x)]
     for dev in peers:
         pl.semaphore_signal(barrier, inc=1, device_id=dev, device_id_type=MESH)
+
+    token_copy = pltpu.make_async_copy(tok_hbm, tok_ref, w_sem.at[0])
+    token_copy.start()
+    weight_copies = [pltpu.make_async_copy(up_hbm, wu, w_sem.at[1])]
+    for part in range(wd.shape[0]):
+        weight_copies.append(
+            pltpu.make_async_copy(
+                down_hbm.at[:, pl.ds(part * lane_group, lane_group)], wd.at[part], w_sem.at[2 + part]
+            )
+        )
+    for copy in weight_copies:
+        copy.start()
 
     sub = lax.broadcasted_iota(jnp.int32, (SLOTS, n_tok), 0)
     lane = lax.broadcasted_iota(jnp.int32, (SLOTS, n_tok), 1)
@@ -74,9 +77,20 @@
     expert_of = y - offset
     expert_of = jnp.where(expert_of < 0, expert_of + n_y, expert_of)
     expert_of = jnp.where(expert_of >= n_y, expert_of - n_y, expert_of).astype(F32)
-    first = meta_ref[0:1, :] == expert_of
-    second = meta_ref[1:2, :] == expert_of
-    share = 1.0 / (1.0 + jnp.exp(-meta_ref[2:3, :]))
+    spread = lax.broadcasted_iota(jnp.int32, (16, n_tok), 1) % 16
+    spread = jnp.where(spread == lax.broadcasted_iota(jnp.int32, (16, n_tok), 0), 1.0, 0.0)
+
+    def as_row(blocks):
+        wide = jnp.dot(
+            jnp.concatenate(blocks, axis=0), spread,
+            preferred_element_type=F32, precision=lax.Precision.HIGHEST,
+        )
+        return jnp.sum(jnp.where(lane // 16 == sub, wide, 0.0), axis=0, keepdims=True)
+
+    micros = range(n_tok // 16)
+    first = as_row([ids_ref[m, 0, 0:1, :].astype(F32) for m in micros]) == expert_of
+    second = as_row([ids_ref[m, 0, 1:2, :].astype(F32) for m in micros]) == expert_of
+    share = 1.0 / (1.0 + jnp.exp(-as_row([gap_ref[m] for m in micros])))
     weight = jnp.where(first, share, 0.0) + jnp.where(second, 1.0 - share, 0.0)
     member = first | second
     before = lax.broadcasted_iota(jnp.int32, (n_tok, n_tok), 0)
@@ -87,24 +101,37 @@
     code = jnp.where(member, rank + ((lane // 16) * CAP).astype(F32), -1.0)
     row_id = lax.broadcasted_iota(jnp.int32, (rows, n_tok), 0).astype(F32)
     lo_half = pl.multiple_of(c * half, 128)
+    token_copy.wait()
     own_half = tok_ref[:, pl.ds(lo_half, half)]
+    gain = jnp.concatenate([gain_ref[i : i + 1, :] for i in range(width // 128)], axis=1)
+    gains = [gain[:, i * lane_half : (i + 1) * lane_half] for i in range(width // lane_half)]
     for k in range(SLOTS):
         hit = code[k : k + 1, :] == row_id
         pick = jnp.where(hit, 1.0, 0.0).astype(BF16)
         if k == 0:
-            both = jnp.dot(pick, tok_ref[...], preferred_element_type=F32).astype(BF16)
-            xg[0, 0] = both[:, :half]
-            xg[1, 0] = both[:, half:]
+            value = jnp.dot(pick, tok_ref[...], preferred_element_type=F32).astype(BF16)
+            for h in range(2):
+                for w in range(4):
+                    lo = h * half + (w % 2) * lane_half
+                    xg[h, 0, w] = value[(w // 2) * row_half : (w // 2 + 1) * row_half, lo : lo + lane_half]
         else:
-            pk[k] = jnp.dot(pick, own_half, preferred_element_type=F32).astype(BF16)
+            value = jnp.dot(pick, own_half, preferred_element_type=F32).astype(BF16)
+            for w in range(4):
+                lo = (w % 2) * lane_half
+                pk[k, w] = value[(w // 2) * row_half : (w // 2 + 1) * row_half, lo : lo + lane_half]
 
     pl.semaphore_wait(barrier, len(peers))
 
-    a_copies = [None]
-    for k in range(1, SLOTS):
-        copy = remote(pk.at[k], xg.at[c, k], a_s.at[k], a_r.at[k], dev_y(-OFFSETS[k]))
-        copy.start()
-        a_copies.append(copy)
+    quarter = z % 4
+    a_copies, h_copies, b_copies = {}, {}, {}
+    for k in (1, 2):
+        a_copies[k] = remote(pk.at[k], xg.at[c, k], a_s.at[k, 0], a_r.at[k, 0], dev_y(-OFFSETS[k]))
+        a_copies[k].start()
+    for k in (7, 5, 6, 3, 4):
+        a_copies[k] = remote(
+            pk.at[k, quarter], xg.at[c, k, quarter], a_s.at[k, 0], a_r.at[k, 0], dev_y(-OFFSETS[k])
+        )
+        a_copies[k].start()
 
     for k in range(SLOTS):
         hit = code[k : k + 1, :] == row_id
@@ -113,42 +140,58 @@
         pwh[pl.ds(k * rows, rows), :] = high
         pwl[pl.ds(k * rows, rows), :] = (placed - high.astype(F32)).astype(BF16)
 
-    b_copies = {}
     c_copies, d_copies, e_copies, f_copies, g_copies = {}, {}, {}, {}, {}
 
-    def prepare(g, q, k, h, total):
-        lo = pl.multiple_of(h * half, 128) if not isinstance(h, int) else h * half
-        block = xg[h, k].astype(F32)
-        total = total + jnp.sum(block * block, axis=-1, keepdims=True)
-        xn[g, pl.ds(q * rows, rows), pl.ds(lo, half)] = (block * gain_ref[:, pl.ds(lo, half)]).astype(BF16)
-        return total
+    def share_far(k):
+        a_copies[k].wait_recv()
+        block = xg.at[c, k, quarter]
+        two_away = 2 * lax.rem(z + 2 + 4 * c, n_z) + c
+        for i, dev in ((1, dev_z(1)), (2, dev_z(7)), (3, (two_away, y, x))):
+            copy = remote(block, block, a_s.at[k, i], a_r.at[k, i], dev)
+            copy.start()
+            h_copies[k, i] = copy
+
+    def to_partner(k):
+        if k > 2:
+            for i in (1, 2, 3):
+                h_copies[k, i].wait_recv()
+        else:
+            a_copies[k].wait_recv()
+        b_copies[k] = remote(xg.at[c, k], xg.at[c, k], b_s.at[k], b_r.at[k], (partner, y, x))
+        b_copies[k].start()
+
+    totals = {}
+
+    def prepare(k, h, own):
+        g, q = k // PER, k % PER
+        for rh in range(2):
+            total = totals.get((k, rh), jnp.zeros((row_half, 1), F32))
+            for lh in range(2):
+                block = xg[h, k, 2 * rh + lh].astype(F32)
+                total = total + jnp.sum(block * block, axis=-1, keepdims=True)
+                if isinstance(h, int):
+                    factor, lo = gains[2 * h + lh], h * half + lh * lane_half
+                else:
+                    factor = jnp.where(h == 0, gains[lh], gains[2 + lh])
+                    lo = pl.multiple_of(h * half + lh * lane_half, 128)
+                xn[g, pl.ds(q * rows + rh * row_half, row_half), pl.ds(lo, lane_half)] = (
+                    block * factor
+                ).astype(BF16)
+            totals[k, rh] = total
+
+    def prepare_other(k):
+        b_copies[k].wait_recv()
+        prepare(k, 1 - c, False)
 
     def stage_a(g):
-        totals = []
-        for q in range(PER):
-            k = g * PER + q
-            total = jnp.zeros((rows, 1), F32)
-            if k > 0:
-                a_copies[k].wait_recv()
-                b_copies[k] = remote(xg.at[c, k], xg.at[c, k], b_s.at[k], b_r.at[k], (partner, y, x))
-                b_copies[k].start()
-                total = prepare(g, q, k, c, total)
-            else:
-                total = prepare(g, q, k, 0, total)
-                total = prepare(g, q, k, 1, total)
-            totals.append(total)
-        for q in range(PER):
-            k = g * PER + q
-            if k > 0:
-                b_copies[k].wait_recv()
-                totals[q] = prepare(g, q, k, 1 - c, totals[q])
         if g == 0:
             weight_copies[0].wait()
         gate = jnp.dot(xn[g], wu[...], preferred_element_type=F32)
         lanes = lax.broadcasted_iota(jnp.int32, (rows, 128), 1)
         for q in range(PER):
             rs[g, q, :, pl.ds(0, units)] = gate[q * rows : (q + 1) * rows].astype(BF16)
-            square = jnp.broadcast_to(totals[q], (rows, 128))
+            both = [jnp.broadcast_to(totals[g * PER + q, rh], (row_half, 128)) for rh in range(2)]
+            square = jnp.concatenate(both, axis=0)
             high = square.astype(BF16).astype(F32)
             rs[g, q, :, pl.ds(units, 128)] = jnp.where(lanes < 64, high, square - high).astype(BF16)
         for j in range(1, 4):
@@ -222,12 +265,33 @@
                 copy.start()
                 g_copies[k] = copy
 
+    prepare(0, 0, True)
+    prepare(0, 1, True)
+    to_partner(1)
+    to_partner(2)
+    prepare(1, c, True)
+    prepare(2, c, True)
+    share_far(3)
+    share_far(4)
+    prepare_other(1)
+    prepare_other(2)
+    share_far(5)
+    share_far(6)
+    to_partner(3)
+    share_far(7)
+    prepare(3, c, True)
+    prepare_other(3)
     stage_a(0)
+    for k in range(PER, SLOTS):
+        to_partner(k)
+        prepare(k, c, True)
+    for k in range(PER, SLOTS):
+        prepare_other(k)
+    stage_a(1)
     stage_b(0)
+    stage_b(1)
     stage_c(0)
     stage_d(0)
-    stage_a(1)
-    stage_b(1)
     stage_c(1)
     stage_d(1)
     stage_e(0)
@@ -239,9 +303,7 @@
     moe = lax.dot_general(pwh[...], back, dims, preferred_element_type=F32)
     moe = moe + lax.dot_general(pwl[...], back, dims, preferred_element_type=F32)
     out_ref[...] = moe
-    for copy in a_copies[1:]:
-        copy.wait_send()
-    for group in (b_copies, c_copies, d_copies, e_copies, f_copies, g_copies):
+    for group in (a_copies, h_copies, b_copies, c_copies, d_copies, e_copies, f_copies, g_copies):
         for copy in group.values():
             copy.wait_send()
 
@@ -257,22 +319,21 @@
     lane_group = PER * feats
     parts = width // lane_group
     flat = tokens.reshape(n_tok, width)
-    ids = expert_ids[:, 0].reshape(n_tok, 2).T.astype(F32)
-    gap = gate_gap[:, 0].reshape(1, n_tok)
-    meta = jnp.concatenate([ids, gap], axis=0)
+    ids = expert_ids.transpose(0, 1, 3, 2)
     vmem = pl.BlockSpec(memory_space=pltpu.VMEM)
     hbm = pl.BlockSpec(memory_space=pl.ANY)
     dma = pltpu.SemaphoreType.DMA
     moe = pl.pallas_call(
         layer_kernel,
         out_shape=jax.ShapeDtypeStruct((n_tok, 128), F32),
-        in_specs=[vmem, vmem, vmem, hbm, hbm],
+        in_specs=[hbm, vmem, vmem, vmem, hbm, hbm],
         out_specs=vmem,
         scratch_shapes=[
+            pltpu.VMEM((n_tok, width), BF16),
             pltpu.VMEM((width, units), BF16),
             pltpu.VMEM((parts, units, lane_group), BF16),
-            pltpu.VMEM((SLOTS, rows, width // 2), BF16),
-            pltpu.VMEM((2, SLOTS, rows, width // 2), BF16),
+            pltpu.VMEM((SLOTS, 4, rows // 2, width // 4), BF16),
+            pltpu.VMEM((2, SLOTS, 4, rows // 2, width // 4), BF16),
             pltpu.VMEM((GROUPS, PER * rows, width), BF16),
             pltpu.VMEM((GROUPS, PER, rows, units + 128), BF16),
             pltpu.VMEM((GROUPS, 4, rows, units + 128), BF16),
@@ -285,8 +346,8 @@
             pltpu.VMEM((SLOTS, rows, 128), BF16),
             pltpu.VMEM((SLOTS * rows, n_tok), BF16),
             pltpu.VMEM((SLOTS * rows, n_tok), BF16),
-            dma((1 + parts,)),
-            dma((SLOTS,)), dma((SLOTS,)),
+            dma((2 + parts,)),
+            dma((SLOTS, 4)), dma((SLOTS, 4)),
             dma((SLOTS,)), dma((SLOTS,)),
             dma((GROUPS, 4)), dma((GROUPS, 4)),
             dma((GROUPS, 4)), dma((GROUPS, 4)),
@@ -298,7 +359,7 @@
             collective_id=0, has_side_effects=True, vmem_limit_bytes=56 * 1024 * 1024
         ),
         name="expert_layer",
-    )(flat, norm_gain.reshape(1, width), meta, up_w[0], down_w[0])
+    )(flat, norm_gain.reshape(width // 128, 128), ids, gate_gap, up_w[0], down_w[0])
     start = lax.axis_index("pipe") * feats
     own = lax.dynamic_slice_in_dim(flat, start, feats, axis=1).astype(F32)
     result = (own + moe[:, :feats]).astype(BF16)

time: 76.3 us -> 65.5 us (0.86)
  Pallas kernels: 69.8 us -> 63.7 us
  other arithmetic: 4.2 us -> 1.57 us
  local copies, waits for them, and re-layouts: 1.97 us -> 0 us
    pallas_call x1, Pallas kernels: 69.8 us -> 63.7 us  [on_device(): pl.pallas_call(layer_kernel, out_shape=jax.ShapeDtypeStruct((n_tok, 128),...]
    unnamed x1 -> x0, other arithmetic: 1.35 us -> none
    reshape x1 -> x0, local copies, waits for them, and re-layouts: 1.3 us -> none  [on_device(): norm_gain.reshape(1, width)]
where the time goes in v2:
time: 65.5 us; the launch traced here: 65.3 us
  Pallas kernels  63.7 us (97%)
  other arithmetic  1.57 us (2%)
    pallas_call x1, Pallas kernels, on_device(): pl.pallas_call(layer_kernel, out_shape=jax.ShapeDtypeStruct((n_tok, 128),...  63.7 us
    convert_element_type x1, other arithmetic, on_device(): result = (own + moe[:, :feats]).astype(BF16)  1.57 us

profile of v2, /device:TPU:1, one launch (start us, length us, event | category | flops | bytes accessed | tf_op | source)
XLA Modules:
  0.0 65.3 jit_solution(526682335837830093)
XLA Ops:
  0.0 63.7 %expert_layer.1 = f32[128,128]{1,0:T(8,128)} custom-call(bf16[128,1536]{1,0:T(8,128)(2,1)} %bitcast.10, f32[12,128]{1,0:T(8,128)} %bitcast.12, s32[8,1,2,16]{3,2,1,0:T(2,128)} %bitcast.13, f32[8,1,16]{2,1,0:T(1,128)} %gap_ref.1, bf16[1536,512]{1,0:T(8,128)(2,1)} %bitcast.8, bf16[512,1536]{1,0:T(8,128)(2,1)} %bitcast.9), custom_call_target="tpu_custom_call" | custom-call | tf_op jit(solution)/shard_map/expert_layer/pallas_call | solution.py:326
  63.7 1.6 %add_convert_fusion = bf16[128,96]{1,0:T(8,128)(2,1)} fusion(f32[128,128]{1,0:T(8,128)} %expert_layer.1, bf16[128,1536]{1,0:T(8,128)(2,1)} %bitcast.11, s32[]{:T(128)S(6)} %select_n.3), kind=kLoop, calls=%fused_computation | loop fusion | flops 36864 | bytes 98308 | tf_op jit(solution)/shard_map/convert_element_type | solution.py:365

commit v3 on v2

--- a/solution.py
+++ b/solution.py
@@ -7,9 +7,9 @@
 
 MESH = pl.DeviceIdType.MESH
 OFFSETS = (0, 1, -1, 2, -2, 3, -3, 4)
-GROUPS = 2
 SLOTS = 8
-PER = 4
+PER = 2
+GROUPS = SLOTS // PER
 CAP = 6
 F32 = jnp.float32
 BF16 = jnp.bfloat16
@@ -35,7 +35,8 @@
     row_half, lane_half = pk.shape[2:]
     units = wu.shape[1]
     feats = width // (2 * n_z)
-    lane_group = PER * feats
+    lane_group = 4 * feats
+    piece_rows = PER * rows // 4
 
     def dev_y(offset):
         return (p, lax.rem(y + offset + n_y, n_y), x)
@@ -187,13 +188,20 @@
         if g == 0:
             weight_copies[0].wait()
         gate = jnp.dot(xn[g], wu[...], preferred_element_type=F32)
-        lanes = lax.broadcasted_iota(jnp.int32, (rows, 128), 1)
-        for q in range(PER):
-            rs[g, q, :, pl.ds(0, units)] = gate[q * rows : (q + 1) * rows].astype(BF16)
-            both = [jnp.broadcast_to(totals[g * PER + q, rh], (row_half, 128)) for rh in range(2)]
-            square = jnp.concatenate(both, axis=0)
-            high = square.astype(BF16).astype(F32)
-            rs[g, q, :, pl.ds(units, 128)] = jnp.where(lanes < 64, high, square - high).astype(BF16)
+        lanes = lax.broadcasted_iota(jnp.int32, (PER * rows, 128), 1)
+        square = jnp.concatenate(
+            [
+                jnp.broadcast_to(totals[k, rh], (row_half, 128))
+                for k in range(g * PER, (g + 1) * PER) for rh in range(2)
+            ],
+            axis=0,
+        )
+        high = square.astype(BF16).astype(F32)
+        square = jnp.where(lanes < 64, high, square - high).astype(BF16)
+        gate = gate.astype(BF16)
+        for q in range(4):
+            rs[g, q, :, pl.ds(0, units)] = gate[q * piece_rows : (q + 1) * piece_rows]
+            rs[g, q, :, pl.ds(units, 128)] = square[q * piece_rows : (q + 1) * piece_rows]
         for j in range(1, 4):
             copy = remote(rs.at[g, lax.rem(x + j, n_x)], rr.at[g, j], c_s.at[g, j], c_r.at[g, j], dev_x(j))
             copy.start()
@@ -216,18 +224,18 @@
     def stage_c(g):
         for j in range(1, 4):
             d_copies[g, j].wait_recv()
-        hidden = hb[g].reshape(PER * rows, units)
+        hidden = hb[g].reshape(4 * piece_rows, units)
         if g == 0:
             for copy in weight_copies[1:]:
                 copy.wait()
-        lanes = lax.broadcasted_iota(jnp.int32, (rows, lane_group), 1)
+        lanes = lax.broadcasted_iota(jnp.int32, (piece_rows, lane_group), 1)
         for part in range(wd.shape[0]):
             outs = jnp.dot(hidden, wd[part], preferred_element_type=F32)
-            for r in range(PER):
+            for r in range(4):
                 packed = None
-                for q in range(PER):
-                    piece = outs[q * rows : (q + 1) * rows]
-                    shift = ((q - r) % PER) * feats
+                for q in range(4):
+                    piece = outs[q * piece_rows : (q + 1) * piece_rows]
+                    shift = ((q - r) % 4) * feats
                     moved = piece if shift == 0 else pltpu.roll(piece, shift, 1)
                     packed = moved if packed is None else jnp.where(lanes >= q * feats, moved, packed)
                 cs[g, r % 2, 2 * part + r // 2] = packed.astype(BF16)
@@ -253,14 +261,16 @@
         for j in (1, 7, 2, 6, 3, 5, 4):
             f_copies[g, j].wait_recv()
             total = total + zr[g, j].astype(F32)
-        for q in reversed(range(PER)):
-            k = g * PER + q
-            moved = total if q == 0 else pltpu.roll(total, lane_group - q * feats, 1)
-            block = moved[:, :128].astype(BF16)
-            if k == 0:
-                ret[0] = block
-            else:
-                ys[k] = block
+        for k in range(g * PER, (g + 1) * PER):
+            for i in range(4 // PER):
+                q = (k % PER) * (4 // PER) + i
+                moved = total if q == 0 else pltpu.roll(total, lane_group - q * feats, 1)
+                block = moved[:, :128].astype(BF16)
+                if k == 0:
+                    ret[k, pl.ds(i * piece_rows, piece_rows)] = block
+                else:
+                    ys[k, pl.ds(i * piece_rows, piece_rows)] = block
+            if k > 0:
                 copy = remote(ys.at[k], ret.at[k], g_s.at[k], g_r.at[k], dev_y(OFFSETS[k]))
                 copy.start()
                 g_copies[k] = copy
@@ -270,32 +280,49 @@
     to_partner(1)
     to_partner(2)
     prepare(1, c, True)
-    prepare(2, c, True)
     share_far(3)
     share_far(4)
     prepare_other(1)
-    prepare_other(2)
+    stage_a(0)
     share_far(5)
     share_far(6)
+    share_far(7)
+    prepare(2, c, True)
+    prepare_other(2)
     to_partner(3)
-    share_far(7)
     prepare(3, c, True)
+    to_partner(4)
     prepare_other(3)
-    stage_a(0)
-    for k in range(PER, SLOTS):
-        to_partner(k)
-        prepare(k, c, True)
-    for k in range(PER, SLOTS):
-        prepare_other(k)
     stage_a(1)
+    to_partner(5)
+    prepare(4, c, True)
+    prepare(5, c, True)
+    prepare_other(4)
+    to_partner(6)
+    to_partner(7)
     stage_b(0)
+    prepare_other(5)
+    stage_a(2)
+    prepare(6, c, True)
+    prepare(7, c, True)
     stage_b(1)
     stage_c(0)
+    prepare_other(6)
+    prepare_other(7)
+    stage_a(3)
     stage_d(0)
+    stage_b(2)
     stage_c(1)
     stage_d(1)
+    stage_b(3)
+    stage_c(2)
+    stage_d(2)
+    stage_c(3)
+    stage_d(3)
     stage_e(0)
     stage_e(1)
+    stage_e(2)
+    stage_e(3)
     for k in range(1, SLOTS):
         g_copies[k].wait_recv()
     back = ret[...].reshape(SLOTS * rows, 128)
@@ -316,7 +343,8 @@
     pipe = lax.axis_size("pipe")
     n_z = pipe // 2
     feats = width // pipe
-    lane_group = PER * feats
+    lane_group = 4 * feats
+    piece_rows = PER * rows // 4
     parts = width // lane_group
     flat = tokens.reshape(n_tok, width)
     ids = expert_ids.transpose(0, 1, 3, 2)
@@ -335,13 +363,13 @@
             pltpu.VMEM((SLOTS, 4, rows // 2, width // 4), BF16),
             pltpu.VMEM((2, SLOTS, 4, rows // 2, width // 4), BF16),
             pltpu.VMEM((GROUPS, PER * rows, width), BF16),
-            pltpu.VMEM((GROUPS, PER, rows, units + 128), BF16),
-            pltpu.VMEM((GROUPS, 4, rows, units + 128), BF16),
-            pltpu.VMEM((GROUPS, PER, rows, units), BF16),
-            pltpu.VMEM((GROUPS, 2, n_z, rows, lane_group), BF16),
-            pltpu.VMEM((GROUPS, n_z, rows, lane_group), BF16),
-            pltpu.VMEM((GROUPS, n_z, rows, lane_group), BF16),
-            pltpu.VMEM((GROUPS, n_z, rows, lane_group), BF16),
+            pltpu.VMEM((GROUPS, 4, piece_rows, units + 128), BF16),
+            pltpu.VMEM((GROUPS, 4, piece_rows, units + 128), BF16),
+            pltpu.VMEM((GROUPS, 4, piece_rows, units), BF16),
+            pltpu.VMEM((GROUPS, 2, n_z, piece_rows, lane_group), BF16),
+            pltpu.VMEM((GROUPS, n_z, piece_rows, lane_group), BF16),
+            pltpu.VMEM((GROUPS, n_z, piece_rows, lane_group), BF16),
+            pltpu.VMEM((GROUPS, n_z, piece_rows, lane_group), BF16),
             pltpu.VMEM((SLOTS, rows, 128), BF16),
             pltpu.VMEM((SLOTS, rows, 128), BF16),
             pltpu.VMEM((SLOTS * rows, n_tok), BF16),

time: 65.5 us -> 60.2 us (0.919)
  Pallas kernels: 63.7 us -> 58.4 us
    pallas_call x1, Pallas kernels: 63.7 us -> 58.4 us  [on_device(): pl.pallas_call(layer_kernel, out_shape=jax.ShapeDtypeStruct((n_tok, 128),...]
where the time goes in v3:
time: 60.2 us; the launch traced here: 60 us
  Pallas kernels  58.4 us (97%)
  other arithmetic  1.57 us (3%)
    pallas_call x1, Pallas kernels, on_device(): pl.pallas_call(layer_kernel, out_shape=jax.ShapeDtypeStruct((n_tok, 128),...  58.4 us
    convert_element_type x1, other arithmetic, on_device(): result = (own + moe[:, :feats]).astype(BF16)  1.57 us

profile of v3, /device:TPU:1, one launch (start us, length us, event | category | flops | bytes accessed | tf_op | source)
XLA Modules:
  0.0 60.0 jit_solution(191163049096316659)
XLA Ops:
  0.0 58.4 %expert_layer.1 = f32[128,128]{1,0:T(8,128)} custom-call(bf16[128,1536]{1,0:T(8,128)(2,1)} %bitcast.10, f32[12,128]{1,0:T(8,128)} %bitcast.12, s32[8,1,2,16]{3,2,1,0:T(2,128)} %bitcast.13, f32[8,1,16]{2,1,0:T(1,128)} %gap_ref.1, bf16[1536,512]{1,0:T(8,128)(2,1)} %bitcast.8, bf16[512,1536]{1,0:T(8,128)(2,1)} %bitcast.9), custom_call_target="tpu_custom_call" | custom-call | tf_op jit(solution)/shard_map/expert_layer/pallas_call | solution.py:354
  58.4 1.6 %add_convert_fusion = bf16[128,96]{1,0:T(8,128)(2,1)} fusion(f32[128,128]{1,0:T(8,128)} %expert_layer.1, bf16[128,1536]{1,0:T(8,128)(2,1)} %bitcast.11, s32[]{:T(128)S(6)} %select_n.3), kind=kLoop, calls=%fused_computation | loop fusion | flops 36864 | bytes 98308 | tf_op jit(solution)/shard_map/convert_element_type | solution.py:393

commit v4 on v3

--- a/solution.py
+++ b/solution.py
@@ -10,14 +10,17 @@
 SLOTS = 8
 PER = 2
 GROUPS = SLOTS // PER
+NEAR = (1, 2)
+FAR = (7, 5, 6, 3, 4)
+RELAYED = (0, 3, 2)
 CAP = 6
 F32 = jnp.float32
 BF16 = jnp.bfloat16
 
 
 def layer_kernel(
-    tok_hbm, gain_ref, ids_ref, gap_ref, up_hbm, down_hbm, out_ref,
-    tok_ref, wu, wd, pk, xg, xn, rs, rr, hb, cs, cr, zs, zr, ys, ret, pwh, pwl,
+    tok_hbm, gain_hbm, ids_hbm, gap_hbm, up_hbm, down_hbm, out_ref,
+    tok_ref, own_ref, gain_ref, ids_ref, gap_ref, wu, wd, pk, xg, xn, rs, rr, hb, cs, cr, zs, zr, ys, ret, pwh, pwl,
     w_sem, a_s, a_r, b_s, b_r, c_s, c_r, d_s, d_r, e_s, e_r, f_s, f_r, g_s, g_r,
 ):
     p = lax.axis_index("pipe")
@@ -58,13 +61,19 @@
     for dev in peers:
         pl.semaphore_signal(barrier, inc=1, device_id=dev, device_id_type=MESH)
 
-    token_copy = pltpu.make_async_copy(tok_hbm, tok_ref, w_sem.at[0])
+    small_copies = [
+        pltpu.make_async_copy(src, dst, w_sem.at[i])
+        for i, (src, dst) in enumerate(((ids_hbm, ids_ref), (gap_hbm, gap_ref), (gain_hbm, gain_ref)))
+    ]
+    token_copy = pltpu.make_async_copy(tok_hbm, tok_ref, w_sem.at[3])
+    for copy in small_copies:
+        copy.start()
     token_copy.start()
-    weight_copies = [pltpu.make_async_copy(up_hbm, wu, w_sem.at[1])]
+    weight_copies = [pltpu.make_async_copy(up_hbm, wu, w_sem.at[4])]
     for part in range(wd.shape[0]):
         weight_copies.append(
             pltpu.make_async_copy(
-                down_hbm.at[:, pl.ds(part * lane_group, lane_group)], wd.at[part], w_sem.at[2 + part]
+                down_hbm.at[:, pl.ds(part * lane_group, lane_group)], wd.at[part], w_sem.at[5 + part]
             )
         )
     for copy in weight_copies:
@@ -89,6 +98,8 @@
         return jnp.sum(jnp.where(lane // 16 == sub, wide, 0.0), axis=0, keepdims=True)
 
     micros = range(n_tok // 16)
+    for copy in small_copies:
+        copy.wait()
     first = as_row([ids_ref[m, 0, 0:1, :].astype(F32) for m in micros]) == expert_of
     second = as_row([ids_ref[m, 0, 1:2, :].astype(F32) for m in micros]) == expert_of
     share = 1.0 / (1.0 + jnp.exp(-as_row([gap_ref[m] for m in micros])))
@@ -125,13 +136,13 @@
 
     quarter = z % 4
     a_copies, h_copies, b_copies = {}, {}, {}
-    for k in (1, 2):
-        a_copies[k] = remote(pk.at[k], xg.at[c, k], a_s.at[k, 0], a_r.at[k, 0], dev_y(-OFFSETS[k]))
-        a_copies[k].start()
-    for k in (7, 5, 6, 3, 4):
+    for k in FAR:
         a_copies[k] = remote(
             pk.at[k, quarter], xg.at[c, k, quarter], a_s.at[k, 0], a_r.at[k, 0], dev_y(-OFFSETS[k])
         )
+        a_copies[k].start()
+    for k in NEAR:
+        a_copies[k] = remote(pk.at[k], xg.at[c, k], a_s.at[k, 0], a_r.at[k, 0], dev_y(-OFFSETS[k]))
         a_copies[k].start()
 
     for k in range(SLOTS):
@@ -140,6 +151,11 @@
         high = placed.astype(BF16)
         pwh[pl.ds(k * rows, rows), :] = high
         pwl[pl.ds(k * rows, rows), :] = (placed - high.astype(F32)).astype(BF16)
+
+    start = p * feats
+    base = pl.multiple_of(jnp.minimum(start // 128 * 128, width - 256), 128)
+    window = tok_ref[:, pl.ds(base, 256)].astype(F32)
+    own_ref[...] = pltpu.roll(window, lax.rem(256 - (start - base), 256), 1)[:, :128]
 
     c_copies, d_copies, e_copies, f_copies, g_copies = {}, {}, {}, {}, {}
 
@@ -153,7 +169,7 @@
             h_copies[k, i] = copy
 
     def to_partner(k):
-        if k > 2:
+        if k in FAR:
             for i in (1, 2, 3):
                 h_copies[k, i].wait_recv()
         else:
@@ -246,21 +262,45 @@
             copy.start()
             e_copies[g, part] = copy
 
+    way = 1 - 2 * c
+
+    def chip(n):
+        return lax.rem(z + way * n + n_z, n_z)
+
+    def partial_sum(g, n):
+        to = chip(n)
+        return cs[g, c, to].astype(F32) + cr[g, to].astype(F32)
+
+    def send_z(g, slot, value, n):
+        zs[g, slot] = value.astype(BF16)
+        dev = (2 * chip(n) + c, y, x)
+        copy = remote(zs.at[g, slot], zr.at[g, slot], f_s.at[g, slot], f_r.at[g, slot], dev)
+        copy.start()
+        f_copies[g, slot] = copy
+
+    def arrived(g, slot):
+        f_copies[g, slot].wait_recv()
+        return zr[g, slot].astype(F32)
+
     def stage_d(g):
         for part in range(wd.shape[0]):
             e_copies[g, part].wait_recv()
-        for j in (4, 3, 5, 2, 6, 1, 7):
-            to = lax.rem(z + j, n_z)
-            zs[g, j] = (cs[g, c, to].astype(F32) + cr[g, to].astype(F32)).astype(BF16)
-            copy = remote(zs.at[g, j], zr.at[g, j], f_s.at[g, j], f_r.at[g, j], dev_z(j))
-            copy.start()
-            f_copies[g, j] = copy
+        if g in RELAYED:
+            for slot, to, via in ((5, 4, 2), (3, 3, 1), (4, -3, -1), (1, 1, 1), (2, -1, -1)):
+                send_z(g, slot, partial_sum(g, to), via)
+        else:
+            for j in (4, 3, 5, 2, 6, 1, 7):
+                send_z(g, j, partial_sum(g, j), j)
+
+    def relay(g):
+        if g in RELAYED:
+            send_z(g, 7, partial_sum(g, -2) + arrived(g, 4), -2)
+            send_z(g, 6, partial_sum(g, 2) + arrived(g, 3) + arrived(g, 5), 2)
 
     def stage_e(g):
-        total = cs[g, c, z].astype(F32) + cr[g, z].astype(F32)
-        for j in (1, 7, 2, 6, 3, 5, 4):
-            f_copies[g, j].wait_recv()
-            total = total + zr[g, j].astype(F32)
+        total = partial_sum(g, 0)
+        for slot in (1, 2, 7, 6) if g in RELAYED else (1, 7, 2, 6, 3, 5, 4):
+            total = total + arrived(g, slot)
         for k in range(g * PER, (g + 1) * PER):
             for i in range(4 // PER):
                 q = (k % PER) * (4 // PER) + i
@@ -277,59 +317,62 @@
 
     prepare(0, 0, True)
     prepare(0, 1, True)
-    to_partner(1)
-    to_partner(2)
-    prepare(1, c, True)
+    share_far(7)
+    share_far(5)
+    share_far(6)
     share_far(3)
     share_far(4)
+    to_partner(1)
+    prepare(1, c, True)
+    to_partner(2)
+    prepare(2, c, True)
     prepare_other(1)
     stage_a(0)
-    share_far(5)
-    share_far(6)
-    share_far(7)
-    prepare(2, c, True)
-    prepare_other(2)
+    to_partner(7)
+    prepare(7, c, True)
+    to_partner(6)
+    prepare(6, c, True)
+    prepare_other(7)
+    prepare_other(6)
+    stage_a(3)
+    to_partner(5)
+    prepare(5, c, True)
+    to_partner(4)
+    prepare(4, c, True)
+    prepare_other(5)
+    prepare_other(4)
+    stage_a(2)
+    stage_b(0)
     to_partner(3)
     prepare(3, c, True)
-    to_partner(4)
     prepare_other(3)
+    prepare_other(2)
     stage_a(1)
-    to_partner(5)
-    prepare(4, c, True)
-    prepare(5, c, True)
-    prepare_other(4)
-    to_partner(6)
-    to_partner(7)
-    stage_b(0)
-    prepare_other(5)
-    stage_a(2)
-    prepare(6, c, True)
-    prepare(7, c, True)
+    stage_b(3)
+    stage_b(2)
+    stage_c(0)
     stage_b(1)
-    stage_c(0)
-    prepare_other(6)
-    prepare_other(7)
-    stage_a(3)
     stage_d(0)
-    stage_b(2)
-    stage_c(1)
-    stage_d(1)
-    stage_b(3)
-    stage_c(2)
-    stage_d(2)
     stage_c(3)
     stage_d(3)
+    stage_c(2)
+    relay(0)
+    stage_d(2)
+    stage_c(1)
+    relay(3)
+    stage_d(1)
     stage_e(0)
+    relay(2)
+    stage_e(3)
+    stage_e(2)
     stage_e(1)
-    stage_e(2)
-    stage_e(3)
     for k in range(1, SLOTS):
         g_copies[k].wait_recv()
     back = ret[...].reshape(SLOTS * rows, 128)
     dims = (((0,), (0,)), ((), ()))
     moe = lax.dot_general(pwh[...], back, dims, preferred_element_type=F32)
     moe = moe + lax.dot_general(pwl[...], back, dims, preferred_element_type=F32)
-    out_ref[...] = moe
+    out_ref[...] = (own_ref[:, :feats] + moe[:, :feats]).astype(BF16)
     for group in (a_copies, h_copies, b_copies, c_copies, d_copies, e_copies, f_copies, g_copies):
         for copy in group.values():
             copy.wait_send()
@@ -351,13 +394,17 @@
     vmem = pl.BlockSpec(memory_space=pltpu.VMEM)
     hbm = pl.BlockSpec(memory_space=pl.ANY)
     dma = pltpu.SemaphoreType.DMA
-    moe = pl.pallas_call(
+    result = pl.pallas_call(
         layer_kernel,
-        out_shape=jax.ShapeDtypeStruct((n_tok, 128), F32),
-        in_specs=[hbm, vmem, vmem, vmem, hbm, hbm],
+        out_shape=jax.ShapeDtypeStruct((n_tok, feats), BF16),
+        in_specs=[hbm] * 6,
         out_specs=vmem,
         scratch_shapes=[
             pltpu.VMEM((n_tok, width), BF16),
+            pltpu.VMEM((n_tok, 128), F32),
+            pltpu.VMEM((width // 128, 128), F32),
+            pltpu.VMEM(ids.shape, jnp.int32),
+            pltpu.VMEM(gate_gap.shape, F32),
             pltpu.VMEM((width, units), BF16),
             pltpu.VMEM((parts, units, lane_group), BF16),
             pltpu.VMEM((SLOTS, 4, rows // 2, width // 4), BF16),
@@ -374,7 +421,7 @@
             pltpu.VMEM((SLOTS, rows, 128), BF16),
             pltpu.VMEM((SLOTS * rows, n_tok), BF16),
             pltpu.VMEM((SLOTS * rows, n_tok), BF16),
-            dma((2 + parts,)),
+            dma((5 + parts,)),
             dma((SLOTS, 4)), dma((SLOTS, 4)),
             dma((SLOTS,)), dma((SLOTS,)),
             dma((GROUPS, 4)), dma((GROUPS, 4)),
@@ -388,9 +435,6 @@
         ),
         name="expert_layer",
     )(flat, norm_gain.reshape(width // 128, 128), ids, gate_gap, up_w[0], down_w[0])
-    start = lax.axis_index("pipe") * feats
-    own = lax.dynamic_slice_in_dim(flat, start, feats, axis=1).astype(F32)
-    result = (own + moe[:, :feats]).astype(BF16)
     return result.reshape(micro, 1, row_count, feats)
 
 

time: 60.2 us -> 56.8 us (0.944)
  Pallas kernels: 58.4 us -> 55.2 us
  other arithmetic: 1.57 us -> 0 us
  local copies, waits for them, and re-layouts: 0 us -> 1.38 us
    pallas_call x1, Pallas kernels: 58.4 us -> 55.2 us  [on_device(): pl.pallas_call(layer_kernel, out_shape=jax.ShapeDtypeStruct((n_tok, feats...]
    convert_element_type x1 -> x0, other arithmetic: 1.57 us -> none  [on_device(): result = (own + moe[:, :feats]).astype(BF16)]
    unnamed x0 -> x1, local copies, waits for them, and re-layouts: none -> 1.38 us
where the time goes in v4:
time: 56.8 us; the launch traced here: 56.6 us
  Pallas kernels  55.2 us (97%)
  local copies, waits for them, and re-layouts  1.38 us (2%)
    pallas_call x1, Pallas kernels, on_device(): pl.pallas_call(layer_kernel, out_shape=jax.ShapeDtypeStruct((n_tok, feats...  55.2 us
    unnamed x1, local copies, waits for them, and re-layouts  1.38 us

profile of v4, /device:TPU:1, one launch (start us, length us, event | category | flops | bytes accessed | tf_op | source)
XLA Modules:
  0.0 56.6 jit_solution(5942683052234604549)
XLA Ops:
  0.0 55.2 %expert_layer.1 = bf16[128,96]{1,0:T(8,128)(2,1)} custom-call(bf16[128,1536]{1,0:T(8,128)(2,1)} %bitcast.10, f32[12,128]{1,0:T(8,128)} %bitcast.12, s32[8,1,2,16]{3,2,1,0:T(2,128)} %bitcast.13, f32[8,1,16]{2,1,0:T(1,128)} %gap_hbm.1, bf16[1536,512]{1,0:T(8,128)(2,1)} %bitcast.8, bf16[512,1536]{1,0:T(8,128)(2,1)} %bitcast.9), custom_call_target="tpu_custom_call" | custom-call | tf_op jit(solution)/shard_map/expert_layer/pallas_call | solution.py:397
  55.2 1.4 %copy.9 = bf16[8,1,16,96]{3,2,1,0:T(8,128)(2,1)} copy(bf16[8,1,16,96]{3,2,1,0:T(8,128)(2,1)} %bitcast.11) | data formatting | bytes 49152

commit v5 on v4

--- a/solution.py
+++ b/solution.py
@@ -10,8 +10,8 @@
 SLOTS = 8
 PER = 2
 GROUPS = SLOTS // PER
-NEAR = (1, 2)
-FAR = (7, 5, 6, 3, 4)
+NEAR = (1, 2, 3, 4)
+FAR = (7, 5, 6)
 RELAYED = (0, 3, 2)
 CAP = 6
 F32 = jnp.float32
@@ -145,12 +145,15 @@
         a_copies[k] = remote(pk.at[k], xg.at[c, k], a_s.at[k, 0], a_r.at[k, 0], dev_y(-OFFSETS[k]))
         a_copies[k].start()
 
+    place = []
     for k in range(SLOTS):
         hit = code[k : k + 1, :] == row_id
         placed = jnp.where(hit, weight[k : k + 1, :], 0.0)
-        high = placed.astype(BF16)
-        pwh[pl.ds(k * rows, rows), :] = high
-        pwl[pl.ds(k * rows, rows), :] = (placed - high.astype(F32)).astype(BF16)
+        place.append(placed)
+    placed = jnp.concatenate(place, axis=0).T
+    high = placed.astype(BF16)
+    pwh[...] = high
+    pwl[...] = (placed - high.astype(F32)).astype(BF16)
 
     start = p * feats
     base = pl.multiple_of(jnp.minimum(start // 128 * 128, width - 256), 128)
@@ -320,8 +323,6 @@
     share_far(7)
     share_far(5)
     share_far(6)
-    share_far(3)
-    share_far(4)
     to_partner(1)
     prepare(1, c, True)
     to_partner(2)
@@ -352,26 +353,25 @@
     stage_b(2)
     stage_c(0)
     stage_b(1)
+    stage_c(3)
     stage_d(0)
-    stage_c(3)
+    stage_c(2)
     stage_d(3)
-    stage_c(2)
+    stage_c(1)
+    stage_d(2)
     relay(0)
-    stage_d(2)
-    stage_c(1)
+    stage_d(1)
     relay(3)
-    stage_d(1)
+    relay(2)
     stage_e(0)
-    relay(2)
     stage_e(3)
     stage_e(2)
     stage_e(1)
     for k in range(1, SLOTS):
         g_copies[k].wait_recv()
     back = ret[...].reshape(SLOTS * rows, 128)
-    dims = (((0,), (0,)), ((), ()))
-    moe = lax.dot_general(pwh[...], back, dims, preferred_element_type=F32)
-    moe = moe + lax.dot_general(pwl[...], back, dims, preferred_element_type=F32)
+    moe = jnp.dot(pwh[...], back, preferred_element_type=F32)
+    moe = moe + jnp.dot(pwl[...], back, preferred_element_type=F32)
     out_ref[...] = (own_ref[:, :feats] + moe[:, :feats]).astype(BF16)
     for group in (a_copies, h_copies, b_copies, c_copies, d_copies, e_copies, f_copies, g_copies):
         for copy in group.values():
@@ -419,8 +419,8 @@
             pltpu.VMEM((GROUPS, n_z, piece_rows, lane_group), BF16),
             pltpu.VMEM((SLOTS, rows, 128), BF16),
             pltpu.VMEM((SLOTS, rows, 128), BF16),
-            pltpu.VMEM((SLOTS * rows, n_tok), BF16),
-            pltpu.VMEM((SLOTS * rows, n_tok), BF16),
+            pltpu.VMEM((n_tok, SLOTS * rows), BF16),
+            pltpu.VMEM((n_tok, SLOTS * rows), BF16),
             dma((5 + parts,)),
             dma((SLOTS, 4)), dma((SLOTS, 4)),
             dma((SLOTS,)), dma((SLOTS,)),

time: 56.8 us -> 56.2 us (0.989)
  Pallas kernels: 55.2 us -> 54.6 us
    pallas_call x1, Pallas kernels: 55.2 us -> 54.6 us  [on_device(): pl.pallas_call(layer_kernel, out_shape=jax.ShapeDtypeStruct((n_tok, feats...]
where the time goes in v5:
time: 56.2 us; the launch traced here: 56 us
  Pallas kernels  54.6 us (97%)
  local copies, waits for them, and re-layouts  1.38 us (2%)
    pallas_call x1, Pallas kernels, on_device(): pl.pallas_call(layer_kernel, out_shape=jax.ShapeDtypeStruct((n_tok, feats...  54.6 us
    unnamed x1, local copies, waits for them, and re-layouts  1.38 us

profile of v5, /device:TPU:1, one launch (start us, length us, event | category | flops | bytes accessed | tf_op | source)
XLA Modules:
  0.0 56.0 jit_solution(17914669639548346886)
XLA Ops:
  0.0 54.6 %expert_layer.1 = bf16[128,96]{1,0:T(8,128)(2,1)} custom-call(bf16[128,1536]{1,0:T(8,128)(2,1)} %bitcast.10, f32[12,128]{1,0:T(8,128)} %bitcast.12, s32[8,1,2,16]{3,2,1,0:T(2,128)} %bitcast.13, f32[8,1,16]{2,1,0:T(1,128)} %gap_hbm.1, bf16[1536,512]{1,0:T(8,128)(2,1)} %bitcast.8, bf16[512,1536]{1,0:T(8,128)(2,1)} %bitcast.9), custom_call_target="tpu_custom_call" | custom-call | tf_op jit(solution)/shard_map/expert_layer/pallas_call | solution.py:397
  54.6 1.4 %copy.9 = bf16[8,1,16,96]{3,2,1,0:T(8,128)(2,1)} copy(bf16[8,1,16,96]{3,2,1,0:T(8,128)(2,1)} %bitcast.11) | data formatting | bytes 49152

commit v6 on v5

--- a/solution.py
+++ b/solution.py
@@ -56,8 +56,10 @@
         )
 
     barrier = pltpu.get_barrier_semaphore()
-    peers = [dev_y(o) for o in OFFSETS[1:]] + [dev_x(j) for j in range(1, 4)]
-    peers += [dev_z(j) for j in range(1, 8)] + [(partner, y, x)]
+    peers = []
+    for o, j in zip(OFFSETS[:0:-1], (4, 3, 5, 2, 6, 1, 7)):
+        peers += [dev_y(o), dev_z(j)]
+    peers += [dev_x(j) for j in (2, 1, 3)] + [(partner, y, x)]
     for dev in peers:
         pl.semaphore_signal(barrier, inc=1, device_id=dev, device_id_type=MESH)
 
@@ -289,7 +291,7 @@
         for part in range(wd.shape[0]):
             e_copies[g, part].wait_recv()
         if g in RELAYED:
-            for slot, to, via in ((5, 4, 2), (3, 3, 1), (4, -3, -1), (1, 1, 1), (2, -1, -1)):
+            for slot, to, via in ((5, 4, 2), (4, -3, -1), (3, 3, 1), (1, 1, 1), (2, -1, -1)):
                 send_z(g, slot, partial_sum(g, to), via)
         else:
             for j in (4, 3, 5, 2, 6, 1, 7):

time: 56.2 us -> 56.1 us (level)
  no operation moved by 1% of the time
where the time goes in v6:
time: 56.1 us; the launch traced here: 55.8 us
  Pallas kernels  54.4 us (97%)
  local copies, waits for them, and re-layouts  1.38 us (2%)
    pallas_call x1, Pallas kernels, on_device(): pl.pallas_call(layer_kernel, out_shape=jax.ShapeDtypeStruct((n_tok, feats...  54.4 us
    unnamed x1, local copies, waits for them, and re-layouts  1.38 us

profile of v6, /device:TPU:1, one launch (start us, length us, event | category | flops | bytes accessed | tf_op | source)
XLA Modules:
  0.0 55.8 jit_solution(5122399085667871193)
XLA Ops:
  0.0 54.4 %expert_layer.1 = bf16[128,96]{1,0:T(8,128)(2,1)} custom-call(bf16[128,1536]{1,0:T(8,128)(2,1)} %bitcast.10, f32[12,128]{1,0:T(8,128)} %bitcast.12, s32[8,1,2,16]{3,2,1,0:T(2,128)} %bitcast.13, f32[8,1,16]{2,1,0:T(1,128)} %gap_hbm.1, bf16[1536,512]{1,0:T(8,128)(2,1)} %bitcast.8, bf16[512,1536]{1,0:T(8,128)(2,1)} %bitcast.9), custom_call_target="tpu_custom_call" | custom-call | tf_op jit(solution)/shard_map/expert_layer/pallas_call | solution.py:399
  54.4 1.4 %copy.9 = bf16[8,1,16,96]{3,2,1,0:T(8,128)(2,1)} copy(bf16[8,1,16,96]{3,2,1,0:T(8,128)(2,1)} %bitcast.11) | data formatting | bytes 49152
